TPU v7x, 512 devices: a whole 4x4x16 slice. The times are simulated.
512 devices in a mesh: freq: 64 (over z, x_hi, core), space: 8 (over x_lo, y).
Axes of the slice: x: 4 (x_hi: 2, x_lo: 2; x = x_hi * 2 + x_lo), y: 4, z: 16, core: 2. Of those that a mesh axis runs over, the one named last changes fastest.
Arguments:
- series: bfloat16 [2048, 131072], P('freq', 'space')
- starts: int32 [7], replicated, may hold values from 0 to 1536, as said below
- freqs: int32 [64], replicated, may hold values from 0 to 511, as said below
- alpha: int32 [1], replicated, may hold values from 1 to 63
Outputs:
- spectra: bfloat16 [64, 2, 7, 131072], P('freq', None, None, 'space')
- gram: float32 [64, 2, 63, 63], P('freq')
Inputs may be any that keep to these rules, and one draw needn't show every extreme that they name: `starts`: increasing; the first is 0, the last 1536; consecutive ones lie 512 / 4 to 384 apart. `freqs`: 64 distinct bins, 0 and 511 among them.
All inputs are finite; a program needn't handle non-finite values.
Results may differ from a plain program's by a relative error of at most 0.005.
Values may be sent and summed in bfloat16 or wider, within the bound.
No kernel may reach another device: no remote copies, remote signals or barrier semaphores. Data moves between devices by JAX's collectives and lax.ppermute only.
A program may use at most 64 MiB of HBM per device.

v0:
```python
import math

import jax
import jax.numpy as jnp
from jax import lax
from jax.sharding import PartitionSpec as P

NFFT = 512
NBLK = 7
HALF = 4
SHIFTS = 9


def transform_table(freqs, alpha):
    sample_index = jnp.arange(NFFT, dtype=jnp.int32)
    shift_index = jnp.arange(SHIFTS, dtype=jnp.int32) - HALF
    freq_bins = jnp.mod(freqs[:, None] + shift_index[None, :] * alpha[0], NFFT)
    phase_steps = jnp.mod(freq_bins[:, :, None] * sample_index[None, None, :], NFFT)
    phase = phase_steps.astype(jnp.float32) * (2.0 * math.pi / NFFT)
    sample_float = sample_index.astype(jnp.float32)
    window_shape = 0.5 - 0.5 * jnp.cos(sample_float * (2.0 * math.pi / NFFT))
    window_scale = window_shape / jnp.sqrt(jnp.sum(window_shape * window_shape))
    real_part = window_scale * jnp.cos(phase)
    imag_part = -(window_scale * jnp.sin(phase))
    return jnp.stack([real_part, imag_part], axis=1).astype(jnp.bfloat16)


def split_quadrants(products, order):
    real_gram = products[..., :order, :order] + products[..., order:, order:]
    imag_gram = products[..., :order, order:] - products[..., order:, :order]
    return jnp.stack([real_gram, imag_gram], axis=-3)


def per_device(series, starts, freqs, alpha):
    slab_cells = series.shape[1]
    total_cells = slab_cells * lax.axis_size("space")
    nfreq = freqs.shape[0]
    order = SHIFTS * NBLK
    local_rows = lax.all_to_all(series, "freq", split_axis=1, concat_axis=0, tiled=True)
    local_cells = local_rows.shape[1]
    flat_table = transform_table(freqs, alpha).reshape(nfreq * 2 * SHIFTS, NFFT)
    blocks = []
    for block in range(NBLK):
        block_rows = lax.dynamic_slice_in_dim(local_rows, starts[block], NFFT, 0)
        spec_block = jnp.dot(flat_table, block_rows, preferred_element_type=jnp.float32)
        blocks.append(spec_block.astype(jnp.bfloat16).reshape(nfreq, 2, SHIFTS, local_cells))
    blockspec = jnp.stack(blocks, axis=3)
    received = lax.all_to_all(blockspec, "freq", split_axis=0, concat_axis=4, tiled=True)
    stacked = received.reshape(2 * order, slab_cells)
    products = lax.dot_general(
        stacked, stacked, (((1,), (1,)), ((), ())), preferred_element_type=jnp.float32
    )
    gram_part = split_quadrants(products, order)[None]
    own_spectra = received[:, :, HALF]
    gram = lax.psum(gram_part, "space") / total_cells
    return (own_spectra, gram)


def solution(mesh):
    placed = (P("freq", "space"), P(), P(), P())
    return jax.shard_map(
        per_device,
        mesh=mesh,
        in_specs=placed,
        out_specs=(P("freq", None, None, "space"), P("freq", None, None, None)),
        check_vma=False,
    )
```

profile of v0, /device:TPU:4, one launch (start us, length us, event | category | flops | bytes accessed | tf_op | source)
XLA Modules:
  0.0 362.7 jit_solution(13131280645304690328)
XLA Ops:
  0.6 2.3 copy.29
  3.0 18.9 %all-to-all-start = ((bf16[32,64,256]{2,0,1:T(8,128)(2,1)}), bf16[32,64,256]{2,0,1:T(8,128)(2,1)}, u32[]{:S(2)}, u32[]{:S(2)}) async-start(bf16[32,64,256]{2,0,1:T(8,128)(2,1)} %bitcast.40), calls=%async_computation | async-start | bytes 2097152 | tf_op jit(solution)/shard_map/all_to_all | solution.py:39
  21.9 0.0 copy-done.4
  21.9 0.7 fusion.24
  31.8 0.6 multiply_reduce_fusion
  33.2 0.0 copy-done.5
  33.3 0.1 add_select_fusion.2
  33.3 5.4 %multiply_convert_fusion = (bf16[64,1,9,512]{3,0,2,1:T(8,128)(2,1)S(1)}, bf16[64,1,9,512]{3,0,2,1:T(8,128)(2,1)S(1)}) fusion(s32[64,9]{0,1:T(8,128)S(1)} %add_select_fusion.2, f32[512]{0:T(512)S(1)} %fusion.16), kind=kLoop, calls=%fused_computation.15 | loop fusion | flops 5603328 | bytes 1184000 | tf_op jit(solution)/shard_map/convert
  38.7 0.1 pad_maximum_fusion
  38.8 0.8 copy.19
  39.6 0.6 convert_element_type.51
  44.5 33.4 %all-to-all-done = bf16[32,64,256]{2,0,1:T(8,128)(2,1)} async-done(((bf16[32,64,256]{2,0,1:T(8,128)(2,1)}), bf16[32,64,256]{2,0,1:T(8,128)(2,1)}, u32[]{:S(2)}, u32[]{:S(2)}) %all-to-all-start) | async-done | bytes 1048608 | tf_op jit(solution)/shard_map/all_to_all | solution.py:39
  77.9 1.5 convolution_convert_fusion.6
  79.4 0.2 stack_reshape.21
  79.6 1.0 constant_dynamic-update-slice_fusion.6
  80.6 1.5 convolution_convert_fusion.5
  82.1 0.2 stack_reshape.22
  82.3 2.3 convolution_convert_fusion.4
  84.7 1.3 stack_reshape.23
  86.0 2.3 convolution_convert_fusion.3
  88.3 2.2 stack_reshape.24
  90.5 2.3 convolution_convert_fusion.2
  92.8 2.1 stack_reshape.25
  94.9 2.3 convolution_convert_fusion.1
  97.2 2.1 stack_reshape.26
  99.3 2.3 convolution_convert_fusion
  101.6 1.3 stack_reshape.27
  102.9 1.1 constant_dynamic-update-slice_fusion.5
  104.0 1.1 constant_dynamic-update-slice_fusion.4
  105.0 0.5 copy-done.1
  105.6 1.0 constant_dynamic-update-slice_fusion.3
  106.6 0.6 copy-done.2
  107.2 1.0 constant_dynamic-update-slice_fusion.2
  108.2 0.6 copy-done.3
  108.8 1.1 constant_dynamic-update-slice_fusion.1
  109.9 1.1 constant_dynamic-update-slice_fusion
  110.9 8.5 %copy.21 = bf16[64,2,9,7,256]{4,1,3,2,0:T(2,128)(2,1)} copy(bf16[64,2,9,7,256]{4,2,1,0,3:T(8,128)(2,1)} %constant_dynamic-update-slice_fusion) | data formatting | bytes 8257536 | tf_op jit(solution)/shard_map/stack | solution.py:47
  119.4 193.4 %all_to_all.37 = bf16[64,2,9,7,256]{4,1,3,2,0:T(2,128)(2,1)S(1)} all-to-all(bf16[64,2,9,7,256]{4,1,3,2,0:T(2,128)(2,1)} %copy.21), channel_id=1, replica_groups=mesh['freq'=64,'space'=8] {'freq'}, dimensions={0} | all-to-all | bytes 8257536 | tf_op jit(solution)/shard_map/all_to_all | solution.py:48
  312.8 0.9 copy.23
  313.7 1.0 copy-done
  314.7 0.6 pad.4
  315.3 2.9 copy.27
  318.2 1.2 fusion.25
  319.5 0.1 fusion.14
  319.6 34.6 %psum.7 = f32[1,2,63,63]{3,2,1,0:T(8,128)S(1)} all-reduce(f32[1,2,63,63]{3,2,1,0:T(8,128)S(1)} %maximum_bitcast_fusion), channel_id=1, replica_groups=mesh['freq'=64,'space'=8] {'space'}, use_global_device_ids=true, to_apply=%region_1.2 | all-reduce | flops 7938 | bytes 63504 | tf_op jit(solution)/shard_map/psum | solution.py:55
  354.2 0.7 copy.24
  354.9 6.7 %copy.26 = bf16[1,64,9,7,1,2,256]{6,5,1,4,3,2,0:T(2,128)(2,1)S(1)} copy(bf16[1,64,9,7,1,2,256]{6,5,4,3,2,1,0:T(2,128)(2,1)} %bitcast.44) | data formatting | bytes 8257536 | tf_op jit(solution)/shard_map/all_to_all | solution.py:48
  361.6 1.1 slice_bitcast_fusion
  (10 shorter events, 0.1 us)
Async XLA Ops:
  3.0 18.9 %copy-start.4 = (s32[7]{0:T(128)S(1)}, s32[7]{0:T(128)}, u32[]{:S(2)}) copy-start(s32[7]{0:T(128)} %param.5) | copy-start | bytes 88
  3.0 30.3 %copy-start.5 = (s32[64]{0:T(128)S(1)}, s32[64]{0:T(128)}, u32[]{:S(2)}) copy-start(s32[64]{0:T(128)} %param.6) | copy-start | bytes 772
  3.0 74.9 %all-to-all-start = ((bf16[32,64,256]{2,0,1:T(8,128)(2,1)}), bf16[32,64,256]{2,0,1:T(8,128)(2,1)}, u32[]{:S(2)}, u32[]{:S(2)}) async-start(bf16[32,64,256]{2,0,1:T(8,128)(2,1)} %bitcast.40), calls=%async_computation | async-start | bytes 2097152 | tf_op jit(solution)/shard_map/all_to_all | solution.py:39
  104.0 1.6 copy-start.1
  105.6 1.6 copy-start.2
  107.2 1.6 copy-start.3
  312.8 1.9 copy-start
where the time goes:
time: 364 us; the launch traced here: 363 us
  blocking collectives  228 us (63%)
  local copies, waits for them, and re-layouts  45.3 us (12%)
  waiting for transfers between devices  33.4 us (9%)
  starting transfers between devices  18.9 us (5%)
  matrix products  15.6 us (4%)
  between operations  15.1 us (4%)
  other arithmetic  6.35 us (2%)
    all_to_all x1, blocking collectives, per_device(): lax.all_to_all(blockspec, 'freq', split_axis=0, concat_axis=4, tiled=True)  193 us
    psum x1, blocking collectives, per_device(): gram = lax.psum(gram_part, 'space') / total_cells  34.6 us
    all_to_all x1, waiting for transfers between devices, per_device(): lax.all_to_all(series, 'freq', split_axis=1, concat_axis=0, tiled=True)  33.4 us
    another operation x9, local copies, waits for them, and re-layouts, per_device(): blockspec = jnp.stack(blocks, axis=3)  19.1 us
    all_to_all x1, starting transfers between devices, per_device(): lax.all_to_all(series, 'freq', split_axis=1, concat_axis=0, tiled=True)  18.9 us
    dot_general x7, matrix products, per_device(): jnp.dot(flat_table, block_rows, preferred_element_type=jnp.float32)  14.3 us
    unnamed x21, local copies, waits for them, and re-layouts  13.2 us
    all_to_all x2, local copies, waits for them, and re-layouts, per_device(): lax.all_to_all(blockspec, 'freq', split_axis=0, concat_axis=4, tiled=True)  7.57 us
  transfers between devices with their start and end apart: 1, of which 1 were waited for; matrix products, arithmetic and copies ran while one was open for 2% of the time, Pallas kernels for 0%

commit v1 on v0

--- a/solution.py
+++ b/solution.py
@@ -9,6 +9,8 @@
 NBLK = 7
 HALF = 4
 SHIFTS = 9
+ORDER = SHIFTS * NBLK
+ENTRIES = 2 * ORDER * ORDER
 
 
 def transform_table(freqs, alpha):
@@ -33,27 +35,40 @@
 
 def per_device(series, starts, freqs, alpha):
     slab_cells = series.shape[1]
-    total_cells = slab_cells * lax.axis_size("space")
-    nfreq = freqs.shape[0]
-    order = SHIFTS * NBLK
-    local_rows = lax.all_to_all(series, "freq", split_axis=1, concat_axis=0, tiled=True)
-    local_cells = local_rows.shape[1]
-    flat_table = transform_table(freqs, alpha).reshape(nfreq * 2 * SHIFTS, NFFT)
+    n_space = lax.axis_size("space")
+    n_freq = freqs.shape[0]
+    total_cells = slab_cells * n_space
+    cells = slab_cells // n_freq
+    piece = -(-ENTRIES // (n_space * 128)) * 128
+
+    rows = lax.all_to_all(series, "freq", split_axis=1, concat_axis=0, tiled=True)
+    flat_table = transform_table(freqs, alpha).reshape(n_freq * 2 * SHIFTS, NFFT)
     blocks = []
     for block in range(NBLK):
-        block_rows = lax.dynamic_slice_in_dim(local_rows, starts[block], NFFT, 0)
+        block_rows = lax.dynamic_slice_in_dim(rows, starts[block], NFFT, 0)
         spec_block = jnp.dot(flat_table, block_rows, preferred_element_type=jnp.float32)
-        blocks.append(spec_block.astype(jnp.bfloat16).reshape(nfreq, 2, SHIFTS, local_cells))
+        blocks.append(spec_block.astype(jnp.bfloat16).reshape(n_freq, 2, SHIFTS, cells))
     blockspec = jnp.stack(blocks, axis=3)
-    received = lax.all_to_all(blockspec, "freq", split_axis=0, concat_axis=4, tiled=True)
-    stacked = received.reshape(2 * order, slab_cells)
-    products = lax.dot_general(
-        stacked, stacked, (((1,), (1,)), ((), ())), preferred_element_type=jnp.float32
-    )
-    gram_part = split_quadrants(products, order)[None]
-    own_spectra = received[:, :, HALF]
-    gram = lax.psum(gram_part, "space") / total_cells
-    return (own_spectra, gram)
+    stacked = blockspec.reshape(n_freq, 2 * ORDER, cells)
+    products = jnp.einsum("jrc,jsc->jrs", stacked, stacked, preferred_element_type=jnp.float32)
+    partial = split_quadrants(products, ORDER).reshape(n_freq, ENTRIES).astype(jnp.bfloat16)
+    partial = jnp.pad(partial, ((0, 0), (0, n_space * piece - ENTRIES)))
+    partial = jnp.transpose(partial.reshape(n_freq, n_space, piece), (1, 0, 2))
+    gathered = lax.all_to_all(partial, "space", split_axis=0, concat_axis=0, tiled=True)
+    slab_sum = jnp.sum(gathered.astype(jnp.float32), axis=0).astype(jnp.bfloat16)
+
+    own = blockspec[:, :, HALF].reshape(n_freq, 2 * NBLK * cells)
+    packed = jnp.concatenate([own, slab_sum], axis=1)
+    packed = packed.reshape(n_freq, packed.shape[1] // 128, 128)
+    received = lax.all_to_all(packed, "freq", split_axis=0, concat_axis=0, tiled=True)
+    received = received.reshape(n_freq, -1)
+    own = received[:, : 2 * NBLK * cells].reshape(n_freq, 2, NBLK, cells)
+    spectra = jnp.transpose(own, (1, 2, 0, 3)).reshape(1, 2, NBLK, slab_cells)
+    gram_piece = jnp.sum(received[:, 2 * NBLK * cells :].astype(jnp.float32), axis=0)
+    spread = jnp.broadcast_to(gram_piece.reshape(1, piece // 128, 128), (n_space, piece // 128, 128))
+    pieces = lax.all_to_all(spread, "space", split_axis=0, concat_axis=0, tiled=True)
+    gram = pieces.reshape(-1)[:ENTRIES].reshape(1, 2, ORDER, ORDER) / total_cells
+    return (spectra, gram)
 
 
 def solution(mesh):

time: 364 us -> 205 us (0.56)
  blocking collectives: 228 us -> 45.3 us
  waiting for transfers between devices: 33.4 us -> 48 us
  starting transfers between devices: 18.9 us -> 27.7 us
  local copies, waits for them, and re-layouts: 45.3 us -> 40.9 us
    all_to_all x1, blocking collectives: 193 us -> 45.3 us  [per_device(): lax.all_to_all(packed, 'freq', split_axis=0, concat_axis=0, tiled=True)]
    psum x1 -> x0, blocking collectives: 34.6 us -> none  [per_device(): gram = lax.psum(gram_part, 'space') / total_cells]
    all_to_all x0 -> x2, waiting for transfers between devices: none -> 14.6 us  [the longest x1 9.93 us: per_device(): lax.all_to_all(partial, 'space', split_axis=0, concat_axis=0, tiled=True)]
    all_to_all x0 -> x2, starting transfers between devices: none -> 8.72 us  [the longest x1 5.09 us: per_device(): lax.all_to_all(partial, 'space', split_axis=0, concat_axis=0, tiled=True)]
    all_to_all x2 -> x0, local copies, waits for them, and re-layouts: 7.57 us -> none  [per_device(): lax.all_to_all(blockspec, 'freq', split_axis=0, concat_axis=4, tiled=True)]
    unnamed x21 -> x18, local copies, waits for them, and re-layouts: 13.2 us -> 8.78 us
  transfers between devices with their start and end apart: 1 -> 3, of which waited for: 1 -> 3; matrix products, arithmetic and copies ran while one was open for 2% -> 7% of each run, Pallas kernels for 0% -> 0%
where the time goes in v1:
time: 205 us; the launch traced here: 204 us
  waiting for transfers between devices  48 us (23%)
  blocking collectives  45.3 us (22%)
  local copies, waits for them, and re-layouts  40.9 us (20%)
  starting transfers between devices  27.7 us (14%)
  matrix products  19 us (9%)
  between operations  15.1 us (7%)
  other arithmetic  8.18 us (4%)
    all_to_all x1, blocking collectives, per_device(): lax.all_to_all(packed, 'freq', split_axis=0, concat_axis=0, tiled=True)  45.3 us
    all_to_all x1, waiting for transfers between devices, per_device(): lax.all_to_all(series, 'freq', split_axis=1, concat_axis=0, tiled=True)  33.4 us
    all_to_all x1, starting transfers between devices, per_device(): lax.all_to_all(series, 'freq', split_axis=1, concat_axis=0, tiled=True)  18.9 us
    another operation x9, local copies, waits for them, and re-layouts, per_device(): blockspec = jnp.stack(blocks, axis=3)  16.4 us
    dot_general x7, matrix products, per_device(): jnp.dot(flat_table, block_rows, preferred_element_type=jnp.float32)  14.3 us
    all_to_all x1, waiting for transfers between devices, per_device(): lax.all_to_all(partial, 'space', split_axis=0, concat_axis=0, tiled=True)  9.93 us
    unnamed x18, local copies, waits for them, and re-layouts  8.78 us
    another operation x1, other arithmetic  5.37 us
  transfers between devices with their start and end apart: 3, of which 3 were waited for; matrix products, arithmetic and copies ran while one was open for 7% of the time, Pallas kernels for 0%

profile of v1, /device:TPU:4, one launch (start us, length us, event | category | flops | bytes accessed | tf_op | source)
XLA Modules:
  0.0 204.1 jit_solution(17525329280515386806)
XLA Ops:
  0.6 2.3 %copy.49 = bf16[4,64,8,256]{3,2,0,1:T(8,128)(2,1)} copy(bf16[4,64,8,256]{3,2,1,0:T(8,128)(2,1)} %bitcast.54) | data formatting | bytes 2097152 | tf_op jit(solution)/shard_map/all_to_all | solution.py:44
  3.0 18.9 %all-to-all-start = ((bf16[32,64,256]{2,0,1:T(8,128)(2,1)}), bf16[32,64,256]{2,0,1:T(8,128)(2,1)}, u32[]{:S(2)}, u32[]{:S(2)}) async-start(bf16[32,64,256]{2,0,1:T(8,128)(2,1)} %bitcast.45), calls=%async_computation | async-start | bytes 2097152 | tf_op jit(solution)/shard_map/all_to_all | solution.py:44
  21.9 0.7 fusion.28
  31.8 0.6 multiply_reduce_fusion
  33.3 5.4 %multiply_convert_fusion = (bf16[64,1,9,512]{3,0,2,1:T(8,128)(2,1)S(1)}, bf16[64,1,9,512]{3,0,2,1:T(8,128)(2,1)S(1)}) fusion(s32[64,9]{0,1:T(8,128)S(1)} %add_select_fusion.2, f32[512]{0:T(512)S(1)} %fusion.20), kind=kLoop, calls=%fused_computation.22 | loop fusion | flops 5603328 | bytes 1184000 | tf_op jit(solution)/shard_map/convert.5
  38.8 0.8 copy.30
  39.6 0.6 convert_element_type.62
  44.5 33.4 %all-to-all-done = bf16[32,64,256]{2,0,1:T(8,128)(2,1)} async-done(((bf16[32,64,256]{2,0,1:T(8,128)(2,1)}), bf16[32,64,256]{2,0,1:T(8,128)(2,1)}, u32[]{:S(2)}, u32[]{:S(2)}) %all-to-all-start) | async-done | bytes 1048608 | tf_op jit(solution)/shard_map/all_to_all | solution.py:44
  77.9 1.5 convolution_convert_fusion.6
  79.6 1.0 constant_dynamic-update-slice_fusion.6
  80.6 1.5 convolution_convert_fusion.5
  82.3 2.3 %convolution_convert_fusion.4 = bf16[1152,256]{1,0:T(8,128)(2,1)} fusion(bf16[1152,512]{1,0:T(8,128)(2,1)S(1)} %convert_element_type.62, bf16[2048,256]{1,0:T(8,128)(2,1)} %bitcast.2, s32[]{:T(128)S(6)} %select_n.53), kind=kOutput, calls=%fused_computation.6 | convolution fusion | flops 302284800 | bytes 2031620 | tf_op jit(solution)/shard_map/dot_general | solution.py:49
  84.7 1.3 stack_reshape.23
  86.0 2.3 %convolution_convert_fusion.3 = bf16[1152,256]{1,0:T(8,128)(2,1)} fusion(bf16[1152,512]{1,0:T(8,128)(2,1)S(1)} %convert_element_type.62, bf16[2048,256]{1,0:T(8,128)(2,1)} %bitcast.2, s32[]{:T(128)S(6)} %select_n.54), kind=kOutput, calls=%fused_computation.5 | convolution fusion | flops 302284800 | bytes 2031620 | tf_op jit(solution)/shard_map/dot_general | solution.py:49
  88.3 2.2 %stack_reshape.24 = bf16[64,2,9,1,256]{4,2,1,0,3:T(8,128)(2,1)} reshape(bf16[1152,256]{1,0:T(8,128)(2,1)} %convolution_convert_fusion.3) | data formatting | bytes 1179648 | tf_op jit(solution)/shard_map/stack;reshape | solution.py:51
  90.5 2.3 %convolution_convert_fusion.2 = bf16[1152,256]{1,0:T(8,128)(2,1)} fusion(bf16[1152,512]{1,0:T(8,128)(2,1)S(1)} %convert_element_type.62, bf16[2048,256]{1,0:T(8,128)(2,1)} %bitcast.2, s32[]{:T(128)S(6)} %select_n.55), kind=kOutput, calls=%fused_computation.4 | convolution fusion | flops 302284800 | bytes 2031620 | tf_op jit(solution)/shard_map/dot_general | solution.py:49
  92.8 2.1 %stack_reshape.25 = bf16[64,2,9,1,256]{4,2,1,0,3:T(8,128)(2,1)} reshape(bf16[1152,256]{1,0:T(8,128)(2,1)} %convolution_convert_fusion.2) | data formatting | bytes 1179648 | tf_op jit(solution)/shard_map/stack;reshape | solution.py:51
  94.9 2.3 %convolution_convert_fusion.1 = bf16[1152,256]{1,0:T(8,128)(2,1)} fusion(bf16[1152,512]{1,0:T(8,128)(2,1)S(1)} %convert_element_type.62, bf16[2048,256]{1,0:T(8,128)(2,1)} %bitcast.2, s32[]{:T(128)S(6)} %select_n.56), kind=kOutput, calls=%fused_computation.3 | convolution fusion | flops 302284800 | bytes 2031620 | tf_op jit(solution)/shard_map/dot_general | solution.py:49
  97.2 2.1 %stack_reshape.26 = bf16[64,2,9,1,256]{4,2,1,0,3:T(8,128)(2,1)} reshape(bf16[1152,256]{1,0:T(8,128)(2,1)} %convolution_convert_fusion.1) | data formatting | bytes 1179648 | tf_op jit(solution)/shard_map/stack;reshape | solution.py:51
  99.3 2.3 %convolution_convert_fusion = bf16[1152,256]{1,0:T(8,128)(2,1)} fusion(bf16[1152,512]{1,0:T(8,128)(2,1)S(1)} %convert_element_type.62, bf16[2048,256]{1,0:T(8,128)(2,1)} %bitcast.2, s32[]{:T(128)S(6)} %select_n.57), kind=kOutput, calls=%fused_computation.2 | convolution fusion | flops 302284800 | bytes 2031620 | tf_op jit(solution)/shard_map/dot_general | solution.py:49
  101.6 1.5 stack_reshape.27
  103.1 1.1 constant_dynamic-update-slice_fusion.5
  104.2 1.1 constant_dynamic-update-slice_fusion.4
  105.2 0.5 copy-done
  105.8 1.0 constant_dynamic-update-slice_fusion.3
  106.8 0.6 copy-done.1
  107.4 1.0 constant_dynamic-update-slice_fusion.2
  108.4 0.6 copy-done.2
  109.0 1.1 constant_dynamic-update-slice_fusion.1
  110.0 1.1 constant_dynamic-update-slice_fusion
  111.1 5.6 %copy.33 = bf16[64,2,9,7,256]{4,0,3,2,1:T(8,128)(2,1)S(1)} copy(bf16[64,2,9,7,256]{4,2,1,0,3:T(8,128)(2,1)} %constant_dynamic-update-slice_fusion) | data formatting | bytes 8257536 | tf_op jit(solution)/shard_map/stack | solution.py:51
  116.7 4.6 %fusion = f32[64,126,126]{2,1,0:T(8,128)S(1)} fusion(bf16[64,126,256]{2,0,1:T(8,128)(2,1)S(1)} %bitcast.48), kind=kOutput, calls=%fused_computation | convolution fusion | flops 520224768 | bytes 8193024 | tf_op jit(solution)/shard_map/jrc,jsc->jrs/dot_general | solution.py:53
  121.4 1.2 fusion.10
  122.6 0.5 pad_maximum_fusion
  123.2 3.3 %convert_element_type.70 = bf16[64,7938]{1,0:T(8,128)(2,1)S(1)} reshape(bf16[64,2,63,63]{3,2,1,0:T(8,128)(2,1)S(1)} %copy.36) | data formatting | bytes 2032128 | tf_op jit(solution)/shard_map/convert_element_type | solution.py:54
  126.6 1.1 copy.48
  127.7 5.1 %all-to-all-start.1 = ((bf16[8,64,1024]{2,1,0:T(8,128)(2,1)}), bf16[8,64,1024]{2,1,0:T(8,128)(2,1)S(1)}, u32[]{:S(2)}, u32[]{:S(2)}) async-start(bf16[8,64,1024]{2,1,0:T(8,128)(2,1)} %bitcast.44), calls=%async_computation.1 | async-start | bytes 2097152 | tf_op jit(solution)/shard_map/all_to_all | solution.py:57
  132.8 3.0 %slice.60 = bf16[64,2,1,7,256]{4,2,1,0,3:T(2,128)(2,1)S(1)} slice(bf16[64,2,9,7,256]{4,2,1,0,3:T(8,128)(2,1)} %constant_dynamic-update-slice_fusion), slice={[0:64], [0:2], [4:5], [0:7], [0:256]} | slice | bytes 917504 | tf_op jit(solution)/shard_map/slice | solution.py:60
  135.8 0.5 copy.32
  136.3 0.5 reshape_squeeze.3
  136.8 9.9 %all-to-all-done.1 = bf16[8,64,1024]{2,1,0:T(8,128)(2,1)S(1)} async-done(((bf16[8,64,1024]{2,1,0:T(8,128)(2,1)}), bf16[8,64,1024]{2,1,0:T(8,128)(2,1)S(1)}, u32[]{:S(2)}, u32[]{:S(2)}) %all-to-all-start.1) | async-done | bytes 1048608 | tf_op jit(solution)/shard_map/all_to_all | solution.py:57
  147.3 45.3 %all_to_all.34 = bf16[64,36,128]{2,1,0:T(8,128)(2,1)S(1)} all-to-all(bf16[64,36,128]{2,1,0:T(8,128)(2,1)S(1)} %reshape.166), channel_id=1, replica_groups=mesh['freq'=64,'space'=8] {'freq'}, dimensions={0} | all-to-all | bytes 1179648 | tf_op jit(solution)/shard_map/all_to_all | solution.py:63
  192.7 0.6 broadcast_in_dim.5
  193.3 3.6 %all-to-all-start.3 = ((f32[8,8,128]{2,1,0:T(8,128)}), f32[8,8,128]{2,1,0:T(8,128)S(1)}, u32[]{:S(2)}, u32[]{:S(2)}) async-start(f32[8,8,128]{2,1,0:T(8,128)} %broadcast_in_dim.5), calls=%async_computation.3 | async-start | bytes 65536 | tf_op jit(solution)/shard_map/all_to_all | solution.py:69
  197.0 0.5 reshape.168
  197.7 0.9 reshape.169
  198.6 4.6 %all-to-all-done.3 = f32[8,8,128]{2,1,0:T(8,128)S(1)} async-done(((f32[8,8,128]{2,1,0:T(8,128)}), f32[8,8,128]{2,1,0:T(8,128)S(1)}, u32[]{:S(2)}, u32[]{:S(2)}) %all-to-all-start.3) | async-done | bytes 32800 | tf_op jit(solution)/shard_map/all_to_all | solution.py:69
  203.4 0.7 copy.39
  (24 shorter events, 2.0 us)
Async XLA Ops:
  3.0 18.9 %copy-start.3 = (s32[7]{0:T(128)S(1)}, s32[7]{0:T(128)}, u32[]{:S(2)}) copy-start(s32[7]{0:T(128)} %param.5) | copy-start | bytes 88
  3.0 30.3 %copy-start.4 = (s32[64]{0:T(128)S(1)}, s32[64]{0:T(128)}, u32[]{:S(2)}) copy-start(s32[64]{0:T(128)} %param.6) | copy-start | bytes 772
  3.0 74.9 %all-to-all-start = ((bf16[32,64,256]{2,0,1:T(8,128)(2,1)}), bf16[32,64,256]{2,0,1:T(8,128)(2,1)}, u32[]{:S(2)}, u32[]{:S(2)}) async-start(bf16[32,64,256]{2,0,1:T(8,128)(2,1)} %bitcast.45), calls=%async_computation | async-start | bytes 2097152 | tf_op jit(solution)/shard_map/all_to_all | solution.py:44
  104.2 1.6 copy-start
  105.8 1.6 copy-start.1
  107.4 1.6 copy-start.2
  127.7 19.0 %all-to-all-start.1 = ((bf16[8,64,1024]{2,1,0:T(8,128)(2,1)}), bf16[8,64,1024]{2,1,0:T(8,128)(2,1)S(1)}, u32[]{:S(2)}, u32[]{:S(2)}) async-start(bf16[8,64,1024]{2,1,0:T(8,128)(2,1)} %bitcast.44), calls=%async_computation.1 | async-start | bytes 2097152 | tf_op jit(solution)/shard_map/all_to_all | solution.py:57
  193.3 9.9 %all-to-all-start.3 = ((f32[8,8,128]{2,1,0:T(8,128)}), f32[8,8,128]{2,1,0:T(8,128)S(1)}, u32[]{:S(2)}, u32[]{:S(2)}) async-start(f32[8,8,128]{2,1,0:T(8,128)} %broadcast_in_dim.5), calls=%async_computation.3 | async-start | bytes 65536 | tf_op jit(solution)/shard_map/all_to_all | solution.py:69

commit v2 on v1

v2 whole, which is shorter than its diff:
```python
import functools
import math

import jax
import jax.numpy as jnp
from jax import lax
from jax.experimental import pallas as pl
from jax.experimental.pallas import tpu as pltpu
from jax.sharding import PartitionSpec as P

NFFT = 512
NBLK = 7
HALF = 4
SHIFTS = 9
ORDER = SHIFTS * NBLK
PAD = 64
LANES = 128
ALIGN = 16
PARTS = 2
OWN = PARTS * NBLK


def transform_table(freqs, alpha):
    sample_index = jnp.arange(NFFT, dtype=jnp.int32)
    shift_index = jnp.arange(SHIFTS, dtype=jnp.int32) - HALF
    freq_bins = jnp.mod(freqs[None, :] + shift_index[:, None] * alpha[0], NFFT)
    phase_steps = jnp.mod(freq_bins[:, :, None] * sample_index[None, None, :], NFFT)
    phase = phase_steps.astype(jnp.float32) * (2.0 * math.pi / NFFT)
    sample_float = sample_index.astype(jnp.float32)
    window_shape = 0.5 - 0.5 * jnp.cos(sample_float * (2.0 * math.pi / NFFT))
    window_scale = window_shape / jnp.sqrt(jnp.sum(window_shape * window_shape))
    real_part = window_scale * jnp.cos(phase)
    imag_part = -(window_scale * jnp.sin(phase))
    return jnp.stack([real_part, imag_part], axis=0).astype(jnp.bfloat16)


def middle_kernel(n_freq, halves, piece_rows, starts_ref, rows_ref, table_ref, own_ref, gram_ref,
                  spec32, own32, gram32):
    span = 2 * PAD
    samples = rows_ref.shape[0]
    zero = jnp.zeros((n_freq, LANES), jnp.float32)
    for half in range(halves):
        for part in range(PARTS):
            spec32[half, pl.ds(part * PAD + ORDER, n_freq, stride=span), :] = zero
    for block in range(NBLK):
        start = starts_ref[block]
        aligned = jnp.minimum(start // ALIGN * ALIGN, samples - NFFT - ALIGN)
        window = rows_ref[pl.ds(pl.multiple_of(aligned, ALIGN), NFFT + ALIGN), :].astype(jnp.float32)
        shifted = pltpu.roll(window, lax.rem(NFFT + ALIGN - (start - aligned), NFFT + ALIGN), 0)
        block_rows = shifted[:NFFT].astype(jnp.bfloat16)
        spec = jnp.dot(table_ref[...], block_rows, preferred_element_type=jnp.float32)
        for part in range(PARTS):
            for shift in range(SHIFTS):
                base = (part * SHIFTS + shift) * n_freq
                row = part * PAD + shift * NBLK + block
                for half in range(halves):
                    values = spec[base : base + n_freq, half * LANES : (half + 1) * LANES]
                    spec32[half, pl.ds(row, n_freq, stride=span), :] = values
                    if shift == HALF:
                        own_row = (part * NBLK + block) * halves + half
                        own32[pl.ds(own_row, n_freq, stride=OWN * halves), :] = values
    own_ref[...] = own32[...].astype(jnp.bfloat16)

    row_index = lax.broadcasted_iota(jnp.int32, (PAD, LANES), 0)
    lane_index = lax.broadcasted_iota(jnp.int32, (PAD, LANES), 1)
    low = lane_index < PAD
    column = jnp.where(low, lane_index, lane_index - PAD)
    keep = (row_index <= column) == low
    sign = jnp.where(low, 1.0, -1.0)
    low_half = low[: PAD // 2]

    def one_frequency(j, carry):
        first = pl.multiple_of(j * span, span)
        stacked = jnp.concatenate(
            [spec32[half, pl.ds(first, span), :] for half in range(halves)], axis=1
        ).astype(jnp.bfloat16)
        products = lax.dot_general(
            stacked, stacked, (((1,), (1,)), ((), ())), preferred_element_type=jnp.float32
        )
        both = products[:PAD] + sign * pltpu.roll(products[PAD:], PAD, 1)
        merged = jnp.where(keep, both, pltpu.roll(both, PAD, 1))
        packed = jnp.where(low_half, merged[: PAD // 2], merged[PAD // 2 :])
        n_piece = (PAD // 2) // piece_rows
        for p in range(n_piece):
            target = p * n_freq * piece_rows + j * piece_rows
            gram32[pl.ds(target, piece_rows), :] = packed[p * piece_rows : (p + 1) * piece_rows]
        return carry

    lax.fori_loop(0, n_freq, one_frequency, 0)
    gram_ref[...] = gram32[...].astype(jnp.bfloat16)


def transform_and_gram(starts, rows, table, n_freq, piece_rows):
    samples, cells = rows.shape
    halves = cells // LANES
    own_rows = n_freq * OWN * halves
    gram_rows = n_freq * (PAD // 2)
    vmem = pl.BlockSpec(memory_space=pltpu.VMEM)
    flops = 2 * NBLK * table.shape[0] * NFFT * cells + 2 * n_freq * (2 * PAD) ** 2 * cells
    return pl.pallas_call(
        functools.partial(middle_kernel, n_freq, halves, piece_rows),
        out_shape=(
            jax.ShapeDtypeStruct((own_rows, LANES), jnp.bfloat16),
            jax.ShapeDtypeStruct((gram_rows, LANES), jnp.bfloat16),
        ),
        in_specs=[pl.BlockSpec(memory_space=pltpu.SMEM), vmem, vmem],
        out_specs=(vmem, vmem),
        scratch_shapes=[
            pltpu.VMEM((halves, n_freq * 2 * PAD, LANES), jnp.float32),
            pltpu.VMEM((own_rows, LANES), jnp.float32),
            pltpu.VMEM((gram_rows, LANES), jnp.float32),
        ],
        cost_estimate=pl.CostEstimate(flops=flops, bytes_accessed=4 << 20, transcendentals=0),
        name="transform_and_gram",
    )(starts, rows, table)


def unpack_gram(packed):
    square = jnp.concatenate([packed[:, :PAD], packed[:, PAD:]], axis=0)[:ORDER, :ORDER]
    upper = jnp.arange(ORDER)[:, None] <= jnp.arange(ORDER)[None, :]
    diagonal = jnp.arange(ORDER)[:, None] == jnp.arange(ORDER)[None, :]
    real_gram = jnp.where(upper, square, square.T)
    imag_gram = jnp.where(upper, jnp.where(diagonal, 0.0, -square.T), square)
    return jnp.stack([real_gram, imag_gram], axis=0)


def per_device(series, starts, freqs, alpha):
    slab_cells = series.shape[1]
    n_space = lax.axis_size("space")
    n_freq = freqs.shape[0]
    total_cells = slab_cells * n_space
    cells = slab_cells // n_freq
    halves = cells // LANES
    piece_rows = (PAD // 2) // n_space

    rows = lax.all_to_all(series, "freq", split_axis=1, concat_axis=0, tiled=True)
    table = transform_table(freqs, alpha).reshape(PARTS * SHIFTS * n_freq, NFFT)
    own, partial = transform_and_gram(starts, rows, table, n_freq, piece_rows)

    partial = partial.reshape(n_space, n_freq * piece_rows, LANES)
    gathered = lax.all_to_all(partial, "space", split_axis=0, concat_axis=0, tiled=True)
    slab_sum = jnp.sum(gathered.astype(jnp.float32), axis=0).astype(jnp.bfloat16)

    packed = jnp.concatenate(
        [own.reshape(n_freq, OWN * halves, LANES), slab_sum.reshape(n_freq, piece_rows, LANES)], axis=1
    )
    received = lax.all_to_all(packed, "freq", split_axis=0, concat_axis=0, tiled=True)
    own = received[:, : OWN * halves].reshape(n_freq, PARTS, NBLK, cells)
    spectra = jnp.transpose(own, (1, 2, 0, 3)).reshape(1, PARTS, NBLK, slab_cells)
    gram_piece = jnp.sum(received[:, OWN * halves :].astype(jnp.float32), axis=0)
    spread = jnp.broadcast_to(gram_piece[None], (n_space, piece_rows, LANES))
    pieces = lax.all_to_all(spread, "space", split_axis=0, concat_axis=0, tiled=True)
    gram = unpack_gram(pieces.reshape(PAD // 2, LANES) / total_cells)[None]
    return (spectra, gram)


def solution(mesh):
    placed = (P("freq", "space"), P(), P(), P())
    return jax.shard_map(
        per_device,
        mesh=mesh,
        in_specs=placed,
        out_specs=(P("freq", None, None, "space"), P("freq", None, None, None)),
        check_vma=False,
    )
```

time: 205 us -> 176 us (0.86)
  the two profiles are of different devices: /device:TPU:4 before, /device:TPU:1 now
where the time goes in v2:
time: 176 us
  waiting for transfers between devices  56.2 us (32%)
  blocking collectives  44.5 us (25%)
  Pallas kernels  31.9 us (18%)
  starting transfers between devices  27.4 us (16%)
  other arithmetic  8.26 us (5%)
  local copies, waits for them, and re-layouts  5.55 us (3%)
  between operations  2.08 us (1%)
    all_to_all x1, waiting for transfers between devices, per_device(): lax.all_to_all(series, 'freq', split_axis=1, concat_axis=0, tiled=True)  45.4 us
    all_to_all x1, blocking collectives, per_device(): lax.all_to_all(packed, 'freq', split_axis=0, concat_axis=0, tiled=True)  44.5 us
    pallas_call x1, Pallas kernels, transform_and_gram(): pl.pallas_call(functools.partial(middle_kernel, n_freq, halves, piece_row...  31.9 us
    all_to_all x1, starting transfers between devices, per_device(): lax.all_to_all(series, 'freq', split_axis=1, concat_axis=0, tiled=True)  19.7 us
    all_to_all x1, waiting for transfers between devices, per_device(): lax.all_to_all(partial, 'space', split_axis=0, concat_axis=0, tiled=True)  7.03 us
    another operation x1, other arithmetic  5.37 us
    all_to_all x1, starting transfers between devices, per_device(): lax.all_to_all(partial, 'space', split_axis=0, concat_axis=0, tiled=True)  4.35 us
    all_to_all x1, waiting for transfers between devices, per_device(): lax.all_to_all(spread, 'space', split_axis=0, concat_axis=0, tiled=True)  3.74 us
  transfers between devices with their start and end apart: 3, of which 3 were waited for; matrix products, arithmetic and copies ran while one was open for 5% of the time, Pallas kernels for 0%

profile of v2, /device:TPU:1, one launch (start us, length us, event | category | flops | bytes accessed | tf_op | source)
XLA Modules:
  0.0 175.9 jit_solution(12962185241118527872)
XLA Ops:
  0.6 2.4 %copy.19 = bf16[4,64,8,256]{3,2,0,1:T(8,128)(2,1)} copy(bf16[4,64,8,256]{3,2,1,0:T(8,128)(2,1)} %bitcast.35) | data formatting | bytes 2097152 | tf_op jit(solution)/shard_map/all_to_all | solution.py:136
  3.0 0.0 copy-start.2
  3.0 19.7 %all-to-all-start = ((bf16[32,64,256]{2,0,1:T(8,128)(2,1)}), bf16[32,64,256]{2,0,1:T(8,128)(2,1)S(1)}, u32[]{:S(2)}, u32[]{:S(2)}) async-start(bf16[32,64,256]{2,0,1:T(8,128)(2,1)} %bitcast.29), calls=%async_computation | async-start | bytes 2097152 | tf_op jit(solution)/shard_map/all_to_all | solution.py:136
  23.4 0.6 multiply_reduce_fusion
  24.8 0.0 copy-done.2
  24.8 0.1 add_select_fusion.2
  24.9 5.4 %multiply_convert_fusion = (bf16[1,9,64,512]{3,2,1,0:T(8,128)(2,1)S(1)}, bf16[1,9,64,512]{3,2,1,0:T(8,128)(2,1)S(1)}) fusion(s32[9,64]{1,0:T(8,128)S(1)} %add_select_fusion.2, f32[512]{0:T(512)S(1)} %fusion.10), kind=kLoop, calls=%fused_computation.8 | loop fusion | flops 5603328 | bytes 1184000 | tf_op jit(solution)/shard_map/convert.1
  30.3 1.1 pad_maximum_fusion
  31.4 45.4 %all-to-all-done = bf16[32,64,256]{2,0,1:T(8,128)(2,1)S(1)} async-done(((bf16[32,64,256]{2,0,1:T(8,128)(2,1)}), bf16[32,64,256]{2,0,1:T(8,128)(2,1)S(1)}, u32[]{:S(2)}, u32[]{:S(2)}) %all-to-all-start) | async-done | bytes 1048608 | tf_op jit(solution)/shard_map/all_to_all | solution.py:136
  76.8 0.0 copy-start
  76.8 1.0 copy-done
  77.8 31.9 %transform_and_gram.1 = (bf16[1792,128]{1,0:T(8,128)(2,1)}, bf16[2048,128]{1,0:T(8,128)(2,1)}) custom-call(s32[7]{0:T(128)} %starts_ref.1, bf16[2048,256]{1,0:T(8,128)(2,1)} %bitcast.36, bf16[1152,512]{1,0:T(8,128)(2,1)} %bitcast.34), custom_call_target="tpu_custom_call" | custom-call | flops 2650800128 | bytes 4194304 | tf_op jit(solution)/shard_map/transform_and_gram/pallas_call | solution.py:100
  109.7 0.0 copy-start.1
  109.7 4.3 %all-to-all-start.1 = ((bf16[8,256,128]{2,1,0:T(8,128)(2,1)}), bf16[8,256,128]{2,1,0:T(8,128)(2,1)S(1)}, u32[]{:S(2)}, u32[]{:S(2)}) async-start(bf16[8,256,128]{2,1,0:T(8,128)(2,1)} %bitcast.37), calls=%async_computation.1 | async-start | bytes 1048576 | tf_op jit(solution)/shard_map/all_to_all | solution.py:141
  114.1 0.0 copy-done.1
  114.1 0.1 reshape.141
  114.2 7.0 %all-to-all-done.1 = bf16[8,256,128]{2,1,0:T(8,128)(2,1)S(1)} async-done(((bf16[8,256,128]{2,1,0:T(8,128)(2,1)}), bf16[8,256,128]{2,1,0:T(8,128)(2,1)S(1)}, u32[]{:S(2)}, u32[]{:S(2)}) %all-to-all-start.1) | async-done | bytes 524320 | tf_op jit(solution)/shard_map/all_to_all | solution.py:141
  121.2 0.1 reduce_sum.31
  121.3 0.1 pad_maximum_fusion.1
  121.4 44.5 %all_to_all.34 = bf16[64,32,128]{2,1,0:T(8,128)(2,1)S(1)} all-to-all(bf16[64,32,128]{2,1,0:T(8,128)(2,1)S(1)} %pad_maximum_fusion.1), channel_id=1, replica_groups=mesh['freq'=64,'space'=8] {'freq'}, dimensions={0} | all-to-all | bytes 1048576 | tf_op jit(solution)/shard_map/all_to_all | solution.py:147
  165.9 0.1 convert_reduce_fusion
  166.0 0.6 broadcast_in_dim.7
  166.6 3.3 %all-to-all-start.3 = ((f32[8,4,128]{2,1,0:T(4,128)}), f32[8,4,128]{2,1,0:T(4,128)S(1)}, u32[]{:S(2)}, u32[]{:S(2)}) async-start(f32[8,4,128]{2,1,0:T(4,128)} %broadcast_in_dim.7), calls=%async_computation.3 | async-start | bytes 32768 | tf_op jit(solution)/shard_map/all_to_all | solution.py:152
  169.9 0.2 reshape.144
  170.1 0.2 copy.14
  170.3 0.9 reshape.145
  171.2 3.7 %all-to-all-done.3 = f32[8,4,128]{2,1,0:T(4,128)S(1)} async-done(((f32[8,4,128]{2,1,0:T(4,128)}), f32[8,4,128]{2,1,0:T(4,128)S(1)}, u32[]{:S(2)}, u32[]{:S(2)}) %all-to-all-start.3) | async-done | bytes 16416 | tf_op jit(solution)/shard_map/all_to_all | solution.py:152
  174.9 0.1 fusion.11
  175.0 0.1 copy.15
  175.2 0.7 maximum_bitcast_fusion
  (7 shorter events, 0.1 us)
Async XLA Ops:
  3.0 21.8 %copy-start.2 = (s32[64]{0:T(128)S(1)}, s32[64]{0:T(128)}, u32[]{:S(2)}) copy-start(s32[64]{0:T(128)} %param.6) | copy-start | bytes 772
  3.0 73.8 %all-to-all-start = ((bf16[32,64,256]{2,0,1:T(8,128)(2,1)}), bf16[32,64,256]{2,0,1:T(8,128)(2,1)S(1)}, u32[]{:S(2)}, u32[]{:S(2)}) async-start(bf16[32,64,256]{2,0,1:T(8,128)(2,1)} %bitcast.29), calls=%async_computation | async-start | bytes 2097152 | tf_op jit(solution)/shard_map/all_to_all | solution.py:136
  76.8 1.0 copy-start
  109.7 4.4 %copy-start.1 = (bf16[1792,128]{1,0:T(8,128)(2,1)S(1)}, bf16[1792,128]{1,0:T(8,128)(2,1)}, u32[]{:S(2)}) copy-start(bf16[1792,128]{1,0:T(8,128)(2,1)} %get-tuple-element.4) | copy-start | bytes 1376260
  109.7 11.5 %all-to-all-start.1 = ((bf16[8,256,128]{2,1,0:T(8,128)(2,1)}), bf16[8,256,128]{2,1,0:T(8,128)(2,1)S(1)}, u32[]{:S(2)}, u32[]{:S(2)}) async-start(bf16[8,256,128]{2,1,0:T(8,128)(2,1)} %bitcast.37), calls=%async_computation.1 | async-start | bytes 1048576 | tf_op jit(solution)/shard_map/all_to_all | solution.py:141
  166.6 8.3 %all-to-all-start.3 = ((f32[8,4,128]{2,1,0:T(4,128)}), f32[8,4,128]{2,1,0:T(4,128)S(1)}, u32[]{:S(2)}, u32[]{:S(2)}) async-start(f32[8,4,128]{2,1,0:T(4,128)} %broadcast_in_dim.7), calls=%async_computation.3 | async-start | bytes 32768 | tf_op jit(solution)/shard_map/all_to_all | solution.py:152

commit v3 on v2

--- a/solution.py
+++ b/solution.py
@@ -15,7 +15,8 @@
 ORDER = SHIFTS * NBLK
 PAD = 64
 LANES = 128
-ALIGN = 16
+SPREAD = 2
+SPAN = 136
 PARTS = 2
 OWN = PARTS * NBLK
 
@@ -35,19 +36,20 @@
 
 
 def middle_kernel(n_freq, halves, piece_rows, starts_ref, rows_ref, table_ref, own_ref, gram_ref,
-                  spec32, own32, gram32):
-    span = 2 * PAD
+                  rows32, spec32, own32, gram32):
     samples = rows_ref.shape[0]
-    zero = jnp.zeros((n_freq, LANES), jnp.float32)
     for half in range(halves):
+        lanes = slice(half * LANES, (half + 1) * LANES)
+        rows32[half, pl.ds(0, samples, stride=SPREAD), :] = rows_ref[:, lanes].astype(jnp.float32)
         for part in range(PARTS):
-            spec32[half, pl.ds(part * PAD + ORDER, n_freq, stride=span), :] = zero
-    for block in range(NBLK):
-        start = starts_ref[block]
-        aligned = jnp.minimum(start // ALIGN * ALIGN, samples - NFFT - ALIGN)
-        window = rows_ref[pl.ds(pl.multiple_of(aligned, ALIGN), NFFT + ALIGN), :].astype(jnp.float32)
-        shifted = pltpu.roll(window, lax.rem(NFFT + ALIGN - (start - aligned), NFFT + ALIGN), 0)
-        block_rows = shifted[:NFFT].astype(jnp.bfloat16)
+            zero = jnp.zeros((n_freq, LANES), jnp.float32)
+            spec32[half, pl.ds(part * PAD + ORDER, n_freq, stride=SPAN), :] = zero
+
+    def one_block(block, carry):
+        first = starts_ref[block] * SPREAD
+        block_rows = jnp.concatenate(
+            [rows32[half, pl.ds(first, NFFT, stride=SPREAD), :] for half in range(halves)], axis=1
+        ).astype(jnp.bfloat16)
         spec = jnp.dot(table_ref[...], block_rows, preferred_element_type=jnp.float32)
         for part in range(PARTS):
             for shift in range(SHIFTS):
@@ -55,10 +57,13 @@
                 row = part * PAD + shift * NBLK + block
                 for half in range(halves):
                     values = spec[base : base + n_freq, half * LANES : (half + 1) * LANES]
-                    spec32[half, pl.ds(row, n_freq, stride=span), :] = values
+                    spec32[half, pl.ds(row, n_freq, stride=SPAN), :] = values
                     if shift == HALF:
                         own_row = (part * NBLK + block) * halves + half
                         own32[pl.ds(own_row, n_freq, stride=OWN * halves), :] = values
+        return carry
+
+    lax.fori_loop(0, NBLK, one_block, 0, unroll=True)
     own_ref[...] = own32[...].astype(jnp.bfloat16)
 
     row_index = lax.broadcasted_iota(jnp.int32, (PAD, LANES), 0)
@@ -70,9 +75,9 @@
     low_half = low[: PAD // 2]
 
     def one_frequency(j, carry):
-        first = pl.multiple_of(j * span, span)
+        first = pl.multiple_of(j * SPAN, 8)
         stacked = jnp.concatenate(
-            [spec32[half, pl.ds(first, span), :] for half in range(halves)], axis=1
+            [spec32[half, pl.ds(first, 2 * PAD), :] for half in range(halves)], axis=1
         ).astype(jnp.bfloat16)
         products = lax.dot_general(
             stacked, stacked, (((1,), (1,)), ((), ())), preferred_element_type=jnp.float32
@@ -80,13 +85,12 @@
         both = products[:PAD] + sign * pltpu.roll(products[PAD:], PAD, 1)
         merged = jnp.where(keep, both, pltpu.roll(both, PAD, 1))
         packed = jnp.where(low_half, merged[: PAD // 2], merged[PAD // 2 :])
-        n_piece = (PAD // 2) // piece_rows
-        for p in range(n_piece):
+        for p in range(PAD // 2 // piece_rows):
             target = p * n_freq * piece_rows + j * piece_rows
             gram32[pl.ds(target, piece_rows), :] = packed[p * piece_rows : (p + 1) * piece_rows]
         return carry
 
-    lax.fori_loop(0, n_freq, one_frequency, 0)
+    lax.fori_loop(0, n_freq, one_frequency, 0, unroll=8)
     gram_ref[...] = gram32[...].astype(jnp.bfloat16)
 
 
@@ -106,11 +110,13 @@
         in_specs=[pl.BlockSpec(memory_space=pltpu.SMEM), vmem, vmem],
         out_specs=(vmem, vmem),
         scratch_shapes=[
-            pltpu.VMEM((halves, n_freq * 2 * PAD, LANES), jnp.float32),
+            pltpu.VMEM((halves, samples * SPREAD, LANES), jnp.float32),
+            pltpu.VMEM((halves, n_freq * SPAN, LANES), jnp.float32),
             pltpu.VMEM((own_rows, LANES), jnp.float32),
             pltpu.VMEM((gram_rows, LANES), jnp.float32),
         ],
         cost_estimate=pl.CostEstimate(flops=flops, bytes_accessed=4 << 20, transcendentals=0),
+        compiler_params=pltpu.CompilerParams(vmem_limit_bytes=28 << 20),
         name="transform_and_gram",
     )(starts, rows, table)
 

time: 176 us -> 151 us (0.86)
  Pallas kernels: 31.9 us -> 8.11 us
    pallas_call x1, Pallas kernels: 31.9 us -> 8.11 us  [transform_and_gram(): pl.pallas_call(functools.partial(middle_kernel, n_freq, halves, piece_row...]
where the time goes in v3:
time: 151 us
  waiting for transfers between devices  57.2 us (38%)
  blocking collectives  44.5 us (29%)
  starting transfers between devices  27.3 us (18%)
  Pallas kernels  8.11 us (5%)
  other arithmetic  7.25 us (5%)
  local copies, waits for them, and re-layouts  4.51 us (3%)
  between operations  2.09 us (1%)
    all_to_all x1, waiting for transfers between devices, per_device(): lax.all_to_all(series, 'freq', split_axis=1, concat_axis=0, tiled=True)  46.4 us
    all_to_all x1, blocking collectives, per_device(): lax.all_to_all(packed, 'freq', split_axis=0, concat_axis=0, tiled=True)  44.5 us
    all_to_all x1, starting transfers between devices, per_device(): lax.all_to_all(series, 'freq', split_axis=1, concat_axis=0, tiled=True)  19.7 us
    pallas_call x1, Pallas kernels, transform_and_gram(): pl.pallas_call(functools.partial(middle_kernel, n_freq, halves, piece_row...  8.11 us
    all_to_all x1, waiting for transfers between devices, per_device(): lax.all_to_all(partial, 'space', split_axis=0, concat_axis=0, tiled=True)  7.04 us
    another operation x1, other arithmetic  5.37 us
    all_to_all x1, starting transfers between devices, per_device(): lax.all_to_all(partial, 'space', split_axis=0, concat_axis=0, tiled=True)  4.2 us
    all_to_all x1, waiting for transfers between devices, per_device(): lax.all_to_all(spread, 'space', split_axis=0, concat_axis=0, tiled=True)  3.74 us
  transfers between devices with their start and end apart: 3, of which 3 were waited for; matrix products, arithmetic and copies ran while one was open for 5% of the time, Pallas kernels for 0%

profile of v3, /device:TPU:1, one launch (start us, length us, event | category | flops | bytes accessed | tf_op | source)
XLA Modules:
  0.0 150.9 jit_solution(11637204050220873384)
XLA Ops:
  0.6 2.3 %copy.19 = bf16[4,64,8,256]{3,2,0,1:T(8,128)(2,1)} copy(bf16[4,64,8,256]{3,2,1,0:T(8,128)(2,1)} %bitcast.36) | data formatting | bytes 2097152 | tf_op jit(solution)/shard_map/all_to_all | solution.py:142
  3.0 0.0 copy-start.1
  3.0 19.7 %all-to-all-start = ((bf16[32,64,256]{2,0,1:T(8,128)(2,1)}), bf16[32,64,256]{2,0,1:T(8,128)(2,1)S(1)}, u32[]{:S(2)}, u32[]{:S(2)}) async-start(bf16[32,64,256]{2,0,1:T(8,128)(2,1)} %bitcast.29), calls=%async_computation | async-start | bytes 2097152 | tf_op jit(solution)/shard_map/all_to_all | solution.py:142
  23.4 0.6 multiply_reduce_fusion
  24.8 0.0 copy-done.1
  24.8 0.1 add_select_fusion.2
  24.9 5.4 %multiply_convert_fusion = (bf16[1,9,64,512]{3,2,1,0:T(8,128)(2,1)S(1)}, bf16[1,9,64,512]{3,2,1,0:T(8,128)(2,1)S(1)}) fusion(s32[9,64]{1,0:T(8,128)S(1)} %add_select_fusion.2, f32[512]{0:T(512)S(1)} %fusion.10), kind=kLoop, calls=%fused_computation.8 | loop fusion | flops 5603328 | bytes 1184000 | tf_op jit(solution)/shard_map/convert.1
  30.2 0.0 copy-start
  30.2 0.1 pad_maximum_fusion
  30.4 46.4 %all-to-all-done = bf16[32,64,256]{2,0,1:T(8,128)(2,1)S(1)} async-done(((bf16[32,64,256]{2,0,1:T(8,128)(2,1)}), bf16[32,64,256]{2,0,1:T(8,128)(2,1)S(1)}, u32[]{:S(2)}, u32[]{:S(2)}) %all-to-all-start) | async-done | bytes 1048608 | tf_op jit(solution)/shard_map/all_to_all | solution.py:142
  76.8 0.0 copy-done
  76.8 8.1 %transform_and_gram.1 = (bf16[1792,128]{1,0:T(8,128)(2,1)S(1)}, bf16[2048,128]{1,0:T(8,128)(2,1)}) custom-call(s32[7]{0:T(128)S(1)} %copy-done, bf16[2048,256]{1,0:T(8,128)(2,1)S(1)} %bitcast.33, bf16[1152,512]{1,0:T(8,128)(2,1)S(1)} %bitcast.32), custom_call_target="tpu_custom_call" | custom-call | flops 2650800128 | bytes 4194304 | tf_op jit(solution)/shard_map/transform_and_gram/pallas_call | solution.py:104
  84.9 4.2 %all-to-all-start.1 = ((bf16[8,256,128]{2,1,0:T(8,128)(2,1)}), bf16[8,256,128]{2,1,0:T(8,128)(2,1)S(1)}, u32[]{:S(2)}, u32[]{:S(2)}) async-start(bf16[8,256,128]{2,1,0:T(8,128)(2,1)} %bitcast.4), calls=%async_computation.1 | async-start | bytes 1048576 | tf_op jit(solution)/shard_map/all_to_all | solution.py:147
  89.1 0.1 reshape.141
  89.2 7.0 %all-to-all-done.1 = bf16[8,256,128]{2,1,0:T(8,128)(2,1)S(1)} async-done(((bf16[8,256,128]{2,1,0:T(8,128)(2,1)}), bf16[8,256,128]{2,1,0:T(8,128)(2,1)S(1)}, u32[]{:S(2)}, u32[]{:S(2)}) %all-to-all-start.1) | async-done | bytes 524320 | tf_op jit(solution)/shard_map/all_to_all | solution.py:147
  96.2 0.1 reduce_sum.31
  96.3 0.1 pad_maximum_fusion.1
  96.4 44.5 %all_to_all.34 = bf16[64,32,128]{2,1,0:T(8,128)(2,1)S(1)} all-to-all(bf16[64,32,128]{2,1,0:T(8,128)(2,1)S(1)} %pad_maximum_fusion.1), channel_id=1, replica_groups=mesh['freq'=64,'space'=8] {'freq'}, dimensions={0} | all-to-all | bytes 1048576 | tf_op jit(solution)/shard_map/all_to_all | solution.py:153
  140.9 0.1 convert_reduce_fusion
  141.0 0.6 broadcast_in_dim.7
  141.6 3.3 %all-to-all-start.3 = ((f32[8,4,128]{2,1,0:T(4,128)}), f32[8,4,128]{2,1,0:T(4,128)S(1)}, u32[]{:S(2)}, u32[]{:S(2)}) async-start(f32[8,4,128]{2,1,0:T(4,128)} %broadcast_in_dim.7), calls=%async_computation.3 | async-start | bytes 32768 | tf_op jit(solution)/shard_map/all_to_all | solution.py:158
  144.9 0.2 reshape.144
  145.2 0.2 copy.14
  145.3 0.9 reshape.145
  146.2 3.7 %all-to-all-done.3 = f32[8,4,128]{2,1,0:T(4,128)S(1)} async-done(((f32[8,4,128]{2,1,0:T(4,128)}), f32[8,4,128]{2,1,0:T(4,128)S(1)}, u32[]{:S(2)}, u32[]{:S(2)}) %all-to-all-start.3) | async-done | bytes 16416 | tf_op jit(solution)/shard_map/all_to_all | solution.py:158
  149.9 0.1 fusion.11
  150.0 0.1 copy.15
  150.2 0.7 maximum_bitcast_fusion
  (7 shorter events, 0.1 us)
Async XLA Ops:
  3.0 21.8 %copy-start.1 = (s32[64]{0:T(128)S(1)}, s32[64]{0:T(128)}, u32[]{:S(2)}) copy-start(s32[64]{0:T(128)} %param.6) | copy-start | bytes 772
  3.0 73.8 %all-to-all-start = ((bf16[32,64,256]{2,0,1:T(8,128)(2,1)}), bf16[32,64,256]{2,0,1:T(8,128)(2,1)S(1)}, u32[]{:S(2)}, u32[]{:S(2)}) async-start(bf16[32,64,256]{2,0,1:T(8,128)(2,1)} %bitcast.29), calls=%async_computation | async-start | bytes 2097152 | tf_op jit(solution)/shard_map/all_to_all | solution.py:142
  30.2 46.5 %copy-start = (s32[7]{0:T(128)S(1)}, s32[7]{0:T(128)}, u32[]{:S(2)}) copy-start(s32[7]{0:T(128)} %starts_ref.1) | copy-start | bytes 88
  84.9 11.3 %all-to-all-start.1 = ((bf16[8,256,128]{2,1,0:T(8,128)(2,1)}), bf16[8,256,128]{2,1,0:T(8,128)(2,1)S(1)}, u32[]{:S(2)}, u32[]{:S(2)}) async-start(bf16[8,256,128]{2,1,0:T(8,128)(2,1)} %bitcast.4), calls=%async_computation.1 | async-start | bytes 1048576 | tf_op jit(solution)/shard_map/all_to_all | solution.py:147
  141.6 8.3 %all-to-all-start.3 = ((f32[8,4,128]{2,1,0:T(4,128)}), f32[8,4,128]{2,1,0:T(4,128)S(1)}, u32[]{:S(2)}, u32[]{:S(2)}) async-start(f32[8,4,128]{2,1,0:T(4,128)} %broadcast_in_dim.7), calls=%async_computation.3 | async-start | bytes 32768 | tf_op jit(solution)/shard_map/all_to_all | solution.py:158

commit v4 on v3

v4 whole, which is shorter than its diff:
```python
import functools
import math

import jax
import jax.numpy as jnp
from jax import lax
from jax.experimental import pallas as pl
from jax.experimental.pallas import tpu as pltpu
from jax.sharding import PartitionSpec as P

NFFT = 512
NBLK = 7
HALF = 4
SHIFTS = 9
ORDER = SHIFTS * NBLK
PAD = 64
LANES = 128
SPREAD = 2
SPAN = 136
PARTS = 2
OWN = PARTS * NBLK


def transform_table(freqs, alpha):
    sample_index = jnp.arange(NFFT, dtype=jnp.int32)
    shift_index = jnp.arange(SHIFTS, dtype=jnp.int32) - HALF
    freq_bins = jnp.mod(freqs[None, :] + shift_index[:, None] * alpha[0], NFFT)
    phase_steps = jnp.mod(freq_bins[:, :, None] * sample_index[None, None, :], NFFT)
    phase = phase_steps.astype(jnp.float32) * (2.0 * math.pi / NFFT)
    sample_float = sample_index.astype(jnp.float32)
    window_shape = 0.5 - 0.5 * jnp.cos(sample_float * (2.0 * math.pi / NFFT))
    window_scale = window_shape / jnp.sqrt(jnp.sum(window_shape * window_shape))
    real_part = window_scale * jnp.cos(phase)
    imag_part = -(window_scale * jnp.sin(phase))
    return jnp.stack([real_part, imag_part], axis=0).astype(jnp.bfloat16)


def middle_kernel(n_out, scalars_ref, mine_ref, other_ref, table_ref, out_ref, rows32, spec32, out32):
    quarters, spread_rows, _ = rows32.shape
    message = out_ref.shape[0] // n_out
    own_rows = OWN * quarters
    run = spread_rows // SPREAD // (2 * n_out)
    core = scalars_ref[NBLK]
    for quarter in range(quarters):
        lanes = slice(quarter * LANES, (quarter + 1) * LANES)
        for source in range(n_out):
            taken = slice(source * run, (source + 1) * run)
            for ref, side in ((mine_ref, core), (other_ref, 1 - core)):
                first = SPREAD * run * (2 * source + side)
                rows32[quarter, pl.ds(first, run, stride=SPREAD), :] = ref[taken, lanes].astype(jnp.float32)
        for part in range(PARTS):
            zero = jnp.zeros((n_out, LANES), jnp.float32)
            spec32[quarter, pl.ds(part * PAD + ORDER, n_out, stride=SPAN), :] = zero

    for block in range(NBLK):
        first = scalars_ref[block] * SPREAD
        block_rows = jnp.concatenate(
            [rows32[quarter, pl.ds(first, NFFT, stride=SPREAD), :] for quarter in range(quarters)], axis=1
        ).astype(jnp.bfloat16)
        spec = jnp.dot(table_ref[...], block_rows, preferred_element_type=jnp.float32)
        for part in range(PARTS):
            for shift in range(SHIFTS):
                base = (part * SHIFTS + shift) * n_out
                row = part * PAD + shift * NBLK + block
                for quarter in range(quarters):
                    values = spec[base : base + n_out, quarter * LANES : (quarter + 1) * LANES]
                    spec32[quarter, pl.ds(row, n_out, stride=SPAN), :] = values
                    if shift == HALF:
                        own_row = (part * NBLK + block) * quarters + quarter
                        out32[pl.ds(own_row, n_out, stride=message), :] = values

    row_index = lax.broadcasted_iota(jnp.int32, (PAD, LANES), 0)
    lane_index = lax.broadcasted_iota(jnp.int32, (PAD, LANES), 1)
    low = lane_index < PAD
    column = jnp.where(low, lane_index, lane_index - PAD)
    keep = (row_index <= column) == low
    sign = jnp.where(low, 1.0, -1.0)
    low_half = low[: PAD // 2]

    def one_frequency(j, carry):
        first = pl.multiple_of(j * SPAN, 8)
        stacked = jnp.concatenate(
            [spec32[quarter, pl.ds(first, 2 * PAD), :] for quarter in range(quarters)], axis=1
        ).astype(jnp.bfloat16)
        products = lax.dot_general(
            stacked, stacked, (((1,), (1,)), ((), ())), preferred_element_type=jnp.float32
        )
        both = products[:PAD] + sign * pltpu.roll(products[PAD:], PAD, 1)
        merged = jnp.where(keep, both, pltpu.roll(both, PAD, 1))
        packed = jnp.where(low_half, merged[: PAD // 2], merged[PAD // 2 :])
        out32[pl.ds(pl.multiple_of(j * message + own_rows, 8), PAD // 2), :] = packed
        return carry

    lax.fori_loop(0, n_out, one_frequency, 0, unroll=8)
    out_ref[...] = out32[...].astype(jnp.bfloat16)


def transform_and_gram(scalars, mine, other, table, n_out):
    run_rows, cells = mine.shape
    quarters = cells // LANES
    out_rows = n_out * (OWN * quarters + PAD // 2)
    vmem = pl.BlockSpec(memory_space=pltpu.VMEM)
    flops = 2 * NBLK * table.shape[0] * NFFT * cells + 2 * n_out * (2 * PAD) ** 2 * cells
    return pl.pallas_call(
        functools.partial(middle_kernel, n_out),
        out_shape=jax.ShapeDtypeStruct((out_rows, LANES), jnp.bfloat16),
        in_specs=[pl.BlockSpec(memory_space=pltpu.SMEM), vmem, vmem, vmem],
        out_specs=vmem,
        scratch_shapes=[
            pltpu.VMEM((quarters, 2 * run_rows * SPREAD, LANES), jnp.float32),
            pltpu.VMEM((quarters, n_out * SPAN, LANES), jnp.float32),
            pltpu.VMEM((out_rows, LANES), jnp.float32),
        ],
        cost_estimate=pl.CostEstimate(flops=flops, bytes_accessed=4 << 20, transcendentals=0),
        compiler_params=pltpu.CompilerParams(vmem_limit_bytes=32 << 20),
        name="transform_and_gram",
    )(scalars, mine, other, table)


def unpack_gram(packed):
    square = jnp.concatenate([packed[:, :PAD], packed[:, PAD:]], axis=0)[:ORDER, :ORDER]
    upper = jnp.arange(ORDER)[:, None] <= jnp.arange(ORDER)[None, :]
    diagonal = jnp.arange(ORDER)[:, None] == jnp.arange(ORDER)[None, :]
    real_gram = jnp.where(upper, square, square.T)
    imag_gram = jnp.where(upper, jnp.where(diagonal, 0.0, -square.T), square)
    return jnp.stack([real_gram, imag_gram], axis=0)


def per_device(series, starts, freqs, alpha):
    slab_cells = series.shape[1]
    n_space = lax.axis_size("space")
    n_freq = freqs.shape[0]
    n_out = n_freq // 2
    total_cells = slab_cells * n_space
    cells = slab_cells // n_out
    quarters = cells // LANES
    core = lax.rem(lax.axis_index("freq"), 2)
    same_core = [[2 * chip + side for chip in range(n_out)] for side in range(2)]

    mine = lax.all_to_all(
        series, "freq", split_axis=1, concat_axis=0, tiled=True, axis_index_groups=same_core
    )
    own_freqs = jnp.where(core == 0, freqs[0::2], freqs[1::2])
    table = transform_table(own_freqs, alpha).reshape(PARTS * SHIFTS * n_out, NFFT)
    scalars = jnp.concatenate([starts, core[None].astype(starts.dtype)])
    mine, table, scalars = lax.optimization_barrier((mine, table, scalars))
    other = lax.ppermute(mine, "freq", [(index, index ^ 1) for index in range(n_freq)])
    message = transform_and_gram(scalars, mine, other, table, n_out).reshape(n_out, -1, LANES)
    received = lax.all_to_all(
        message, "freq", split_axis=0, concat_axis=0, tiled=True, axis_index_groups=same_core
    )
    own = received[:, : OWN * quarters].reshape(n_out, PARTS, NBLK, cells)
    spectra = jnp.transpose(own, (1, 2, 0, 3)).reshape(1, PARTS, NBLK, slab_cells)
    slab_gram = jnp.sum(received[:, OWN * quarters :].astype(jnp.float32), axis=0)
    spread = jnp.broadcast_to(slab_gram[None], (n_space, PAD // 2, LANES))
    slabs = lax.all_to_all(spread, "space", split_axis=0, concat_axis=0, tiled=True)
    gram = unpack_gram(jnp.sum(slabs, axis=0) / total_cells)[None]
    return (spectra, gram)


def solution(mesh):
    placed = (P("freq", "space"), P(), P(), P())
    return jax.shard_map(
        per_device,
        mesh=mesh,
        in_specs=placed,
        out_specs=(P("freq", None, None, "space"), P("freq", None, None, None)),
        check_vma=False,
    )
```

time: 151 us -> 147 us (0.974)
  the two profiles are of different devices: /device:TPU:1 before, /device:TPU:4 now
where the time goes in v4:
time: 147 us; the launch traced here: 146 us
  waiting for transfers between devices  54.3 us (37%)
  blocking collectives  47 us (32%)
  starting transfers between devices  25.2 us (17%)
  local copies, waits for them, and re-layouts  7.12 us (5%)
  Pallas kernels  6.82 us (5%)
  other arithmetic  3.77 us (3%)
  between operations  2.1 us (1%)
    all_to_all x1, blocking collectives, per_device(): lax.all_to_all(message, 'freq', split_axis=0, concat_axis=0, tiled=True,...  47 us
    all_to_all x1, waiting for transfers between devices, per_device(): lax.all_to_all(series, 'freq', split_axis=1, concat_axis=0, tiled=True, a...  46.9 us
    all_to_all x1, starting transfers between devices, per_device(): lax.all_to_all(series, 'freq', split_axis=1, concat_axis=0, tiled=True, a...  18.2 us
    pallas_call x1, Pallas kernels, transform_and_gram(): pl.pallas_call(functools.partial(middle_kernel, n_out), out_shape=jax.Sha...  6.82 us
    all_to_all x1, starting transfers between devices, per_device(): lax.all_to_all(spread, 'space', split_axis=0, concat_axis=0, tiled=True)  5.13 us
    all_to_all x1, waiting for transfers between devices, per_device(): lax.all_to_all(spread, 'space', split_axis=0, concat_axis=0, tiled=True)  4.82 us
  transfers between devices with their start and end apart: 3, of which 3 were waited for; matrix products, arithmetic and copies ran while one was open for 4% of the time, Pallas kernels for 0%

profile of v4, /device:TPU:4, one launch (start us, length us, event | category | flops | bytes accessed | tf_op | source)
XLA Modules:
  0.0 146.4 jit_solution(12261083778263408428)
XLA Ops:
  0.6 2.3 %copy.23 = bf16[4,32,8,512]{3,2,0,1:T(8,128)(2,1)} copy(bf16[4,32,8,512]{3,2,1,0:T(8,128)(2,1)} %bitcast.39) | data formatting | bytes 2097152 | tf_op jit(solution)/shard_map/all_to_all | solution.py:140
  3.0 18.2 %all-to-all-start = ((bf16[32,32,512]{2,0,1:T(8,128)(2,1)}), bf16[32,32,512]{2,0,1:T(8,128)(2,1)S(1)}, u32[]{:S(2)}, u32[]{:S(2)}) async-start(bf16[32,32,512]{2,0,1:T(8,128)(2,1)} %bitcast.32), calls=%async_computation | async-start | bytes 2097152 | tf_op jit(solution)/shard_map/all_to_all | solution.py:140
  21.2 0.0 copy-start
  21.2 0.6 copy-done
  21.8 0.1 slice.22
  22.0 0.1 slice.21
  22.1 0.7 multiply_reduce_fusion
  24.1 0.0 copy-start.1
  24.1 0.6 copy-done.1
  24.8 0.1 pad_add_fusion.scalars_ref
  24.9 0.1 add_select_fusion.2
  25.0 2.7 %multiply_convert_fusion = (bf16[1,9,32,512]{3,2,1,0:T(8,128)(2,1)S(1)}, bf16[1,9,32,512]{3,2,1,0:T(8,128)(2,1)S(1)}) fusion(s32[9,32]{1,0:T(8,128)S(1)} %add_select_fusion.2, f32[512]{0:T(512)S(1)} %fusion.11), kind=kLoop, calls=%fused_computation.9 | loop fusion | flops 2801664 | bytes 593024 | tf_op jit(solution)/shard_map/convert
  27.7 0.1 pad_maximum_fusion
  27.8 46.9 %all-to-all-done = bf16[32,32,512]{2,0,1:T(8,128)(2,1)S(1)} async-done(((bf16[32,32,512]{2,0,1:T(8,128)(2,1)}), bf16[32,32,512]{2,0,1:T(8,128)(2,1)S(1)}, u32[]{:S(2)}, u32[]{:S(2)}) %all-to-all-start) | async-done | bytes 1048608 | tf_op jit(solution)/shard_map/all_to_all | solution.py:140
  74.7 1.9 %collective-permute-start = (bf16[1024,512]{1,0:T(8,128)(2,1)S(1)}, bf16[1024,512]{1,0:T(8,128)(2,1)S(1)}, u32[]{:S(2)}, u32[]{:S(2)}) collective-permute-start(bf16[1024,512]{1,0:T(8,128)(2,1)S(1)} %bitcast.34), channel_id=1, source_target_pairs={{0,8},{8,0},{16,24},{24,16},{32,40},{40,32},{48,56},{56,48},{64,72... | collective-permute-start | bytes 3145736 | tf_op jit(solution)/shard_map/ppermute | solution.py:147
  76.6 2.6 %collective-permute-done.other_ref = bf16[1024,512]{1,0:T(8,128)(2,1)S(1)} collective-permute-done((bf16[1024,512]{1,0:T(8,128)(2,1)S(1)}, bf16[1024,512]{1,0:T(8,128)(2,1)S(1)}, u32[]{:S(2)}, u32[]{:S(2)}) %collective-permute-start) | collective-permute-done | bytes 1048608 | tf_op jit(solution)/shard_map/ppermute | solution.py:147
  79.2 6.8 %transform_and_gram.1 = bf16[2816,128]{1,0:T(8,128)(2,1)S(1)} custom-call(s32[8]{0:T(128)S(1)} %pad_add_fusion.scalars_ref, bf16[1024,512]{1,0:T(8,128)(2,1)S(1)} %bitcast.35, bf16[1024,512]{1,0:T(8,128)(2,1)S(1)} %collective-permute-done.other_ref, bf16[576,512]{1,0:T(8,128)(2,1)S(1)} %bitcast.37), custom_call_target="tpu_custom_call" | custom-call | flops 2650800128 | bytes 4194304 | tf_op jit(solution)/shard_map/transform_and_gram/pallas_call | solution.py:104
  86.0 47.0 %all_to_all.29 = bf16[32,88,128]{2,1,0:T(8,128)(2,1)S(1)} all-to-all(bf16[32,88,128]{2,1,0:T(8,128)(2,1)S(1)} %bitcast.36), channel_id=1, replica_groups={{0,16,32,48,64,80,96,112,128,144,160,176,192,208,224,240,256,272,288,30..., dimensions={0} | all-to-all | bytes 1441792 | tf_op jit(solution)/shard_map/all_to_all | solution.py:149
  133.1 0.6 broadcast_in_dim.10
  133.8 5.1 %all-to-all-start.2 = ((f32[8,32,128]{2,1,0:T(8,128)}), f32[8,32,128]{2,1,0:T(8,128)S(1)}, u32[]{:S(2)}, u32[]{:S(2)}) async-start(f32[8,32,128]{2,1,0:T(8,128)} %broadcast_in_dim.10), calls=%async_computation.2 | async-start | bytes 262144 | tf_op jit(solution)/shard_map/all_to_all | solution.py:156
  138.9 0.3 reshape.133
  139.3 0.3 copy.18
  139.6 1.1 reshape.134
  140.6 4.8 %all-to-all-done.2 = f32[8,32,128]{2,1,0:T(8,128)S(1)} async-done(((f32[8,32,128]{2,1,0:T(8,128)}), f32[8,32,128]{2,1,0:T(8,128)S(1)}, u32[]{:S(2)}, u32[]{:S(2)}) %all-to-all-start.2) | async-done | bytes 131104 | tf_op jit(solution)/shard_map/all_to_all | solution.py:156
  145.5 0.1 fusion.12
  145.6 0.1 copy.19
  145.7 0.7 copy.20
  (10 shorter events, 0.2 us)
Async XLA Ops:
  3.0 71.7 %all-to-all-start = ((bf16[32,32,512]{2,0,1:T(8,128)(2,1)}), bf16[32,32,512]{2,0,1:T(8,128)(2,1)S(1)}, u32[]{:S(2)}, u32[]{:S(2)}) async-start(bf16[32,32,512]{2,0,1:T(8,128)(2,1)} %bitcast.32), calls=%async_computation | async-start | bytes 2097152 | tf_op jit(solution)/shard_map/all_to_all | solution.py:140
  21.2 0.7 copy-start
  24.1 0.7 copy-start.1
  74.7 4.5 %collective-permute-start = (bf16[1024,512]{1,0:T(8,128)(2,1)S(1)}, bf16[1024,512]{1,0:T(8,128)(2,1)S(1)}, u32[]{:S(2)}, u32[]{:S(2)}) collective-permute-start(bf16[1024,512]{1,0:T(8,128)(2,1)S(1)} %bitcast.34), channel_id=1, source_target_pairs={{0,8},{8,0},{16,24},{24,16},{32,40},{40,32},{48,56},{56,48},{64,72... | collective-permute-start | bytes 3145736 | tf_op jit(solution)/shard_map/ppermute | solution.py:147
  133.8 11.7 %all-to-all-start.2 = ((f32[8,32,128]{2,1,0:T(8,128)}), f32[8,32,128]{2,1,0:T(8,128)S(1)}, u32[]{:S(2)}, u32[]{:S(2)}) async-start(f32[8,32,128]{2,1,0:T(8,128)} %broadcast_in_dim.10), calls=%async_computation.2 | async-start | bytes 262144 | tf_op jit(solution)/shard_map/all_to_all | solution.py:156

commit v5 on v4

--- a/solution.py
+++ b/solution.py
@@ -153,6 +153,7 @@
     spectra = jnp.transpose(own, (1, 2, 0, 3)).reshape(1, PARTS, NBLK, slab_cells)
     slab_gram = jnp.sum(received[:, OWN * quarters :].astype(jnp.float32), axis=0)
     spread = jnp.broadcast_to(slab_gram[None], (n_space, PAD // 2, LANES))
+    spread, spectra = lax.optimization_barrier((spread, spectra))
     slabs = lax.all_to_all(spread, "space", split_axis=0, concat_axis=0, tiled=True)
     gram = unpack_gram(jnp.sum(slabs, axis=0) / total_cells)[None]
     return (spectra, gram)

time: 147 us -> 148 us (level)
  blocking collectives: 47 us -> 58.5 us
  starting transfers between devices: 25.2 us -> 20.1 us
  waiting for transfers between devices: 54.3 us -> 49.5 us
    all_to_all x0 -> x1, blocking collectives: none -> 11.5 us  [per_device(): lax.all_to_all(spread, 'space', split_axis=0, concat_axis=0, tiled=True)]
    all_to_all x1 -> x0, starting transfers between devices: 5.13 us -> none  [per_device(): lax.all_to_all(spread, 'space', split_axis=0, concat_axis=0, tiled=True)]
    all_to_all x1 -> x0, waiting for transfers between devices: 4.82 us -> none  [per_device(): lax.all_to_all(spread, 'space', split_axis=0, concat_axis=0, tiled=True)]
  transfers between devices with their start and end apart: 3 -> 2, of which waited for: 3 -> 2; matrix products, arithmetic and copies ran while one was open for 4% -> 3% of each run, Pallas kernels for 0% -> 0%
where the time goes in v5:
time: 148 us; the launch traced here: 147 us
  blocking collectives  58.5 us (40%)
  waiting for transfers between devices  49.5 us (33%)
  starting transfers between devices  20.1 us (14%)
  Pallas kernels  6.82 us (5%)
  local copies, waits for them, and re-layouts  6.5 us (4%)
  other arithmetic  3.77 us (3%)
  between operations  2.1 us (1%)
    all_to_all x1, blocking collectives, per_device(): lax.all_to_all(message, 'freq', split_axis=0, concat_axis=0, tiled=True,...  47 us
    all_to_all x1, waiting for transfers between devices, per_device(): lax.all_to_all(series, 'freq', split_axis=1, concat_axis=0, tiled=True, a...  46.9 us
    all_to_all x1, starting transfers between devices, per_device(): lax.all_to_all(series, 'freq', split_axis=1, concat_axis=0, tiled=True, a...  18.2 us
    all_to_all x1, blocking collectives, per_device(): lax.all_to_all(spread, 'space', split_axis=0, concat_axis=0, tiled=True)  11.5 us
    pallas_call x1, Pallas kernels, transform_and_gram(): pl.pallas_call(functools.partial(middle_kernel, n_out), out_shape=jax.Sha...  6.82 us
  transfers between devices with their start and end apart: 2, of which 2 were waited for; matrix products, arithmetic and copies ran while one was open for 3% of the time, Pallas kernels for 0%

profile of v5, /device:TPU:4, one launch (start us, length us, event | category | flops | bytes accessed | tf_op | source)
XLA Modules:
  0.0 147.3 jit_solution(11819308516146092241)
XLA Ops:
  0.6 2.4 %copy.23 = bf16[4,32,8,512]{3,2,0,1:T(8,128)(2,1)} copy(bf16[4,32,8,512]{3,2,1,0:T(8,128)(2,1)} %bitcast.39) | data formatting | bytes 2097152 | tf_op jit(solution)/shard_map/all_to_all | solution.py:140
  3.0 18.2 %all-to-all-start = ((bf16[32,32,512]{2,0,1:T(8,128)(2,1)}), bf16[32,32,512]{2,0,1:T(8,128)(2,1)S(1)}, u32[]{:S(2)}, u32[]{:S(2)}) async-start(bf16[32,32,512]{2,0,1:T(8,128)(2,1)} %bitcast.32), calls=%async_computation | async-start | bytes 2097152 | tf_op jit(solution)/shard_map/all_to_all | solution.py:140
  21.2 0.0 copy-start
  21.2 0.6 copy-done
  21.9 0.1 slice.22
  22.0 0.1 slice.21
  22.1 0.7 multiply_reduce_fusion
  24.1 0.0 copy-start.1
  24.1 0.6 copy-done.1
  24.8 0.1 pad_add_fusion.scalars_ref
  24.9 0.1 add_select_fusion.2
  25.0 2.7 %multiply_convert_fusion = (bf16[1,9,32,512]{3,2,1,0:T(8,128)(2,1)S(1)}, bf16[1,9,32,512]{3,2,1,0:T(8,128)(2,1)S(1)}) fusion(s32[9,32]{1,0:T(8,128)S(1)} %add_select_fusion.2, f32[512]{0:T(512)S(1)} %fusion.11), kind=kLoop, calls=%fused_computation.9 | loop fusion | flops 2801664 | bytes 593024 | tf_op jit(solution)/shard_map/convert
  27.7 0.1 pad_maximum_fusion
  27.8 46.9 %all-to-all-done = bf16[32,32,512]{2,0,1:T(8,128)(2,1)S(1)} async-done(((bf16[32,32,512]{2,0,1:T(8,128)(2,1)}), bf16[32,32,512]{2,0,1:T(8,128)(2,1)S(1)}, u32[]{:S(2)}, u32[]{:S(2)}) %all-to-all-start) | async-done | bytes 1048608 | tf_op jit(solution)/shard_map/all_to_all | solution.py:140
  74.7 1.9 %collective-permute-start = (bf16[1024,512]{1,0:T(8,128)(2,1)S(1)}, bf16[1024,512]{1,0:T(8,128)(2,1)S(1)}, u32[]{:S(2)}, u32[]{:S(2)}) collective-permute-start(bf16[1024,512]{1,0:T(8,128)(2,1)S(1)} %bitcast.34), channel_id=1, source_target_pairs={{0,8},{8,0},{16,24},{24,16},{32,40},{40,32},{48,56},{56,48},{64,72... | collective-permute-start | bytes 3145736 | tf_op jit(solution)/shard_map/ppermute | solution.py:147
  76.6 2.6 %collective-permute-done.other_ref = bf16[1024,512]{1,0:T(8,128)(2,1)S(1)} collective-permute-done((bf16[1024,512]{1,0:T(8,128)(2,1)S(1)}, bf16[1024,512]{1,0:T(8,128)(2,1)S(1)}, u32[]{:S(2)}, u32[]{:S(2)}) %collective-permute-start) | collective-permute-done | bytes 1048608 | tf_op jit(solution)/shard_map/ppermute | solution.py:147
  79.2 6.8 %transform_and_gram.1 = bf16[2816,128]{1,0:T(8,128)(2,1)S(1)} custom-call(s32[8]{0:T(128)S(1)} %pad_add_fusion.scalars_ref, bf16[1024,512]{1,0:T(8,128)(2,1)S(1)} %bitcast.35, bf16[1024,512]{1,0:T(8,128)(2,1)S(1)} %collective-permute-done.other_ref, bf16[576,512]{1,0:T(8,128)(2,1)S(1)} %bitcast.37), custom_call_target="tpu_custom_call" | custom-call | flops 2650800128 | bytes 4194304 | tf_op jit(solution)/shard_map/transform_and_gram/pallas_call | solution.py:104
  86.1 47.0 %all_to_all.29 = bf16[32,88,128]{2,1,0:T(8,128)(2,1)S(1)} all-to-all(bf16[32,88,128]{2,1,0:T(8,128)(2,1)S(1)} %bitcast.36), channel_id=1, replica_groups={{0,16,32,48,64,80,96,112,128,144,160,176,192,208,224,240,256,272,288,30..., dimensions={0} | all-to-all | bytes 1441792 | tf_op jit(solution)/shard_map/all_to_all | solution.py:149
  133.1 0.3 reshape.133
  133.5 0.3 copy.18
  133.8 1.1 reshape.134
  134.9 11.5 %all_to_all.30 = f32[8,32,128]{2,1,0:T(8,128)S(1)} all-to-all(f32[8,32,128]{2,1,0:T(8,128)S(1)} %broadcast_in_dim.10), channel_id=1, replica_groups=mesh['freq'=64,'space'=8] {'space'}, dimensions={0} | all-to-all | bytes 262144 | tf_op jit(solution)/shard_map/all_to_all | solution.py:157
  146.4 0.1 fusion.12
  146.5 0.1 copy.19
  146.6 0.7 copy.20
  (11 shorter events, 0.2 us)
Async XLA Ops:
  3.0 71.7 %all-to-all-start = ((bf16[32,32,512]{2,0,1:T(8,128)(2,1)}), bf16[32,32,512]{2,0,1:T(8,128)(2,1)S(1)}, u32[]{:S(2)}, u32[]{:S(2)}) async-start(bf16[32,32,512]{2,0,1:T(8,128)(2,1)} %bitcast.32), calls=%async_computation | async-start | bytes 2097152 | tf_op jit(solution)/shard_map/all_to_all | solution.py:140
  21.2 0.7 copy-start
  24.1 0.7 copy-start.1
  74.7 4.5 %collective-permute-start = (bf16[1024,512]{1,0:T(8,128)(2,1)S(1)}, bf16[1024,512]{1,0:T(8,128)(2,1)S(1)}, u32[]{:S(2)}, u32[]{:S(2)}) collective-permute-start(bf16[1024,512]{1,0:T(8,128)(2,1)S(1)} %bitcast.34), channel_id=1, source_target_pairs={{0,8},{8,0},{16,24},{24,16},{32,40},{40,32},{48,56},{56,48},{64,72... | collective-permute-start | bytes 3145736 | tf_op jit(solution)/shard_map/ppermute | solution.py:147

commit v6 on v4

--- a/solution.py
+++ b/solution.py
@@ -35,9 +35,8 @@
     return jnp.stack([real_part, imag_part], axis=0).astype(jnp.bfloat16)
 
 
-def middle_kernel(n_out, scalars_ref, mine_ref, other_ref, table_ref, out_ref, rows32, spec32, out32):
+def middle_kernel(n_out, scalars_ref, mine_ref, other_ref, table_ref, out_ref, rows32, spec32, own32):
     quarters, spread_rows, _ = rows32.shape
-    message = out_ref.shape[0] // n_out
     own_rows = OWN * quarters
     run = spread_rows // SPREAD // (2 * n_out)
     core = scalars_ref[NBLK]
@@ -67,7 +66,7 @@
                     spec32[quarter, pl.ds(row, n_out, stride=SPAN), :] = values
                     if shift == HALF:
                         own_row = (part * NBLK + block) * quarters + quarter
-                        out32[pl.ds(own_row, n_out, stride=message), :] = values
+                        own32[pl.ds(own_row, n_out, stride=own_rows), :] = values
 
     row_index = lax.broadcasted_iota(jnp.int32, (PAD, LANES), 0)
     lane_index = lax.broadcasted_iota(jnp.int32, (PAD, LANES), 1)
@@ -88,28 +87,28 @@
         both = products[:PAD] + sign * pltpu.roll(products[PAD:], PAD, 1)
         merged = jnp.where(keep, both, pltpu.roll(both, PAD, 1))
         packed = jnp.where(low_half, merged[: PAD // 2], merged[PAD // 2 :])
-        out32[pl.ds(pl.multiple_of(j * message + own_rows, 8), PAD // 2), :] = packed
+        own = own32[pl.ds(pl.multiple_of(j * own_rows, 8), own_rows), :]
+        out_ref[j] = jnp.concatenate([own, packed], axis=0).astype(jnp.bfloat16)
         return carry
 
-    lax.fori_loop(0, n_out, one_frequency, 0, unroll=8)
-    out_ref[...] = out32[...].astype(jnp.bfloat16)
+    lax.fori_loop(0, n_out, one_frequency, 0, unroll=16)
 
 
 def transform_and_gram(scalars, mine, other, table, n_out):
     run_rows, cells = mine.shape
     quarters = cells // LANES
-    out_rows = n_out * (OWN * quarters + PAD // 2)
+    own_rows = OWN * quarters
     vmem = pl.BlockSpec(memory_space=pltpu.VMEM)
     flops = 2 * NBLK * table.shape[0] * NFFT * cells + 2 * n_out * (2 * PAD) ** 2 * cells
     return pl.pallas_call(
         functools.partial(middle_kernel, n_out),
-        out_shape=jax.ShapeDtypeStruct((out_rows, LANES), jnp.bfloat16),
+        out_shape=jax.ShapeDtypeStruct((n_out, own_rows + PAD // 2, LANES), jnp.bfloat16),
         in_specs=[pl.BlockSpec(memory_space=pltpu.SMEM), vmem, vmem, vmem],
         out_specs=vmem,
         scratch_shapes=[
             pltpu.VMEM((quarters, 2 * run_rows * SPREAD, LANES), jnp.float32),
             pltpu.VMEM((quarters, n_out * SPAN, LANES), jnp.float32),
-            pltpu.VMEM((out_rows, LANES), jnp.float32),
+            pltpu.VMEM((n_out * own_rows, LANES), jnp.float32),
         ],
         cost_estimate=pl.CostEstimate(flops=flops, bytes_accessed=4 << 20, transcendentals=0),
         compiler_params=pltpu.CompilerParams(vmem_limit_bytes=32 << 20),
@@ -145,7 +144,7 @@
     scalars = jnp.concatenate([starts, core[None].astype(starts.dtype)])
     mine, table, scalars = lax.optimization_barrier((mine, table, scalars))
     other = lax.ppermute(mine, "freq", [(index, index ^ 1) for index in range(n_freq)])
-    message = transform_and_gram(scalars, mine, other, table, n_out).reshape(n_out, -1, LANES)
+    message = transform_and_gram(scalars, mine, other, table, n_out)
     received = lax.all_to_all(
         message, "freq", split_axis=0, concat_axis=0, tiled=True, axis_index_groups=same_core
     )

time: 147 us -> 146 us (level)
  no operation moved by 1% of the time
where the time goes in v6:
time: 146 us
  waiting for transfers between devices  54.3 us (37%)
  blocking collectives  47 us (32%)
  starting transfers between devices  25.2 us (17%)
  local copies, waits for them, and re-layouts  7.12 us (5%)
  Pallas kernels  6.16 us (4%)
  other arithmetic  3.77 us (3%)
  between operations  2.1 us (1%)
    all_to_all x1, blocking collectives, per_device(): lax.all_to_all(message, 'freq', split_axis=0, concat_axis=0, tiled=True,...  47 us
    all_to_all x1, waiting for transfers between devices, per_device(): lax.all_to_all(series, 'freq', split_axis=1, concat_axis=0, tiled=True, a...  46.9 us
    all_to_all x1, starting transfers between devices, per_device(): lax.all_to_all(series, 'freq', split_axis=1, concat_axis=0, tiled=True, a...  18.2 us
    pallas_call x1, Pallas kernels, transform_and_gram(): pl.pallas_call(functools.partial(middle_kernel, n_out), out_shape=jax.Sha...  6.16 us
    all_to_all x1, starting transfers between devices, per_device(): lax.all_to_all(spread, 'space', split_axis=0, concat_axis=0, tiled=True)  5.11 us
    all_to_all x1, waiting for transfers between devices, per_device(): lax.all_to_all(spread, 'space', split_axis=0, concat_axis=0, tiled=True)  4.82 us
  transfers between devices with their start and end apart: 3, of which 3 were waited for; matrix products, arithmetic and copies ran while one was open for 4% of the time, Pallas kernels for 0%

profile of v6, /device:TPU:4, one launch (start us, length us, event | category | flops | bytes accessed | tf_op | source)
XLA Modules:
  0.0 145.7 jit_solution(9113777933403732293)
XLA Ops:
  0.6 2.3 %copy.23 = bf16[4,32,8,512]{3,2,0,1:T(8,128)(2,1)} copy(bf16[4,32,8,512]{3,2,1,0:T(8,128)(2,1)} %bitcast.37) | data formatting | bytes 2097152 | tf_op jit(solution)/shard_map/all_to_all | solution.py:139
  3.0 18.2 %all-to-all-start = ((bf16[32,32,512]{2,0,1:T(8,128)(2,1)}), bf16[32,32,512]{2,0,1:T(8,128)(2,1)S(1)}, u32[]{:S(2)}, u32[]{:S(2)}) async-start(bf16[32,32,512]{2,0,1:T(8,128)(2,1)} %bitcast.31), calls=%async_computation | async-start | bytes 2097152 | tf_op jit(solution)/shard_map/all_to_all | solution.py:139
  21.2 0.0 copy-start
  21.2 0.6 copy-done
  21.8 0.1 slice.22
  22.0 0.1 slice.21
  22.1 0.7 multiply_reduce_fusion
  24.1 0.0 copy-start.1
  24.1 0.6 copy-done.1
  24.8 0.1 pad_add_fusion.scalars_ref
  24.9 0.1 add_select_fusion.2
  25.0 2.7 %multiply_convert_fusion = (bf16[1,9,32,512]{3,2,1,0:T(8,128)(2,1)S(1)}, bf16[1,9,32,512]{3,2,1,0:T(8,128)(2,1)S(1)}) fusion(s32[9,32]{1,0:T(8,128)S(1)} %add_select_fusion.2, f32[512]{0:T(512)S(1)} %fusion.11), kind=kLoop, calls=%fused_computation.9 | loop fusion | flops 2801664 | bytes 593024 | tf_op jit(solution)/shard_map/convert
  27.7 0.1 pad_maximum_fusion
  27.8 46.9 %all-to-all-done = bf16[32,32,512]{2,0,1:T(8,128)(2,1)S(1)} async-done(((bf16[32,32,512]{2,0,1:T(8,128)(2,1)}), bf16[32,32,512]{2,0,1:T(8,128)(2,1)S(1)}, u32[]{:S(2)}, u32[]{:S(2)}) %all-to-all-start) | async-done | bytes 1048608 | tf_op jit(solution)/shard_map/all_to_all | solution.py:139
  74.7 1.9 %collective-permute-start = (bf16[1024,512]{1,0:T(8,128)(2,1)S(1)}, bf16[1024,512]{1,0:T(8,128)(2,1)S(1)}, u32[]{:S(2)}, u32[]{:S(2)}) collective-permute-start(bf16[1024,512]{1,0:T(8,128)(2,1)S(1)} %bitcast.33), channel_id=1, source_target_pairs={{0,8},{8,0},{16,24},{24,16},{32,40},{40,32},{48,56},{56,48},{64,72... | collective-permute-start | bytes 3145736 | tf_op jit(solution)/shard_map/ppermute | solution.py:146
  76.6 2.6 %collective-permute-done.other_ref = bf16[1024,512]{1,0:T(8,128)(2,1)S(1)} collective-permute-done((bf16[1024,512]{1,0:T(8,128)(2,1)S(1)}, bf16[1024,512]{1,0:T(8,128)(2,1)S(1)}, u32[]{:S(2)}, u32[]{:S(2)}) %collective-permute-start) | collective-permute-done | bytes 1048608 | tf_op jit(solution)/shard_map/ppermute | solution.py:146
  79.2 6.2 %transform_and_gram.1 = bf16[32,88,128]{2,1,0:T(8,128)(2,1)S(1)} custom-call(s32[8]{0:T(128)S(1)} %pad_add_fusion.scalars_ref, bf16[1024,512]{1,0:T(8,128)(2,1)S(1)} %bitcast.34, bf16[1024,512]{1,0:T(8,128)(2,1)S(1)} %collective-permute-done.other_ref, bf16[576,512]{1,0:T(8,128)(2,1)S(1)} %bitcast.35), custom_call_target="tpu_custom_call" | custom-call | flops 2650800128 | bytes 4194304 | tf_op jit(solution)/shard_map/transform_and_gram/pallas_call | solution.py:103
  85.4 47.0 %all_to_all.29 = bf16[32,88,128]{2,1,0:T(8,128)(2,1)S(1)} all-to-all(bf16[32,88,128]{2,1,0:T(8,128)(2,1)S(1)} %transform_and_gram.1), channel_id=1, replica_groups={{0,16,32,48,64,80,96,112,128,144,160,176,192,208,224,240,256,272,288,30..., dimensions={0} | all-to-all | bytes 1441792 | tf_op jit(solution)/shard_map/all_to_all | solution.py:148
  132.5 0.6 broadcast_in_dim.10
  133.1 5.1 %all-to-all-start.2 = ((f32[8,32,128]{2,1,0:T(8,128)}), f32[8,32,128]{2,1,0:T(8,128)S(1)}, u32[]{:S(2)}, u32[]{:S(2)}) async-start(f32[8,32,128]{2,1,0:T(8,128)} %broadcast_in_dim.10), calls=%async_computation.2 | async-start | bytes 262144 | tf_op jit(solution)/shard_map/all_to_all | solution.py:155
  138.3 0.3 reshape.129
  138.6 0.3 copy.18
  138.9 1.1 reshape.130
  140.0 4.8 %all-to-all-done.2 = f32[8,32,128]{2,1,0:T(8,128)S(1)} async-done(((f32[8,32,128]{2,1,0:T(8,128)}), f32[8,32,128]{2,1,0:T(8,128)S(1)}, u32[]{:S(2)}, u32[]{:S(2)}) %all-to-all-start.2) | async-done | bytes 131104 | tf_op jit(solution)/shard_map/all_to_all | solution.py:155
  144.8 0.1 fusion.12
  144.9 0.1 copy.19
  145.0 0.7 copy.20
  (10 shorter events, 0.2 us)
Async XLA Ops:
  3.0 71.7 %all-to-all-start = ((bf16[32,32,512]{2,0,1:T(8,128)(2,1)}), bf16[32,32,512]{2,0,1:T(8,128)(2,1)S(1)}, u32[]{:S(2)}, u32[]{:S(2)}) async-start(bf16[32,32,512]{2,0,1:T(8,128)(2,1)} %bitcast.31), calls=%async_computation | async-start | bytes 2097152 | tf_op jit(solution)/shard_map/all_to_all | solution.py:139
  21.2 0.7 copy-start
  24.1 0.7 copy-start.1
  74.7 4.5 %collective-permute-start = (bf16[1024,512]{1,0:T(8,128)(2,1)S(1)}, bf16[1024,512]{1,0:T(8,128)(2,1)S(1)}, u32[]{:S(2)}, u32[]{:S(2)}) collective-permute-start(bf16[1024,512]{1,0:T(8,128)(2,1)S(1)} %bitcast.33), channel_id=1, source_target_pairs={{0,8},{8,0},{16,24},{24,16},{32,40},{40,32},{48,56},{56,48},{64,72... | collective-permute-start | bytes 3145736 | tf_op jit(solution)/shard_map/ppermute | solution.py:146
  133.1 11.7 %all-to-all-start.2 = ((f32[8,32,128]{2,1,0:T(8,128)}), f32[8,32,128]{2,1,0:T(8,128)S(1)}, u32[]{:S(2)}, u32[]{:S(2)}) async-start(f32[8,32,128]{2,1,0:T(8,128)} %broadcast_in_dim.10), calls=%async_computation.2 | async-start | bytes 262144 | tf_op jit(solution)/shard_map/all_to_all | solution.py:155

commit v7 on v6

--- a/solution.py
+++ b/solution.py
@@ -150,10 +150,10 @@
     )
     own = received[:, : OWN * quarters].reshape(n_out, PARTS, NBLK, cells)
     spectra = jnp.transpose(own, (1, 2, 0, 3)).reshape(1, PARTS, NBLK, slab_cells)
-    slab_gram = jnp.sum(received[:, OWN * quarters :].astype(jnp.float32), axis=0)
+    slab_gram = jnp.sum(received[:, OWN * quarters :].astype(jnp.float32), axis=0).astype(jnp.bfloat16)
     spread = jnp.broadcast_to(slab_gram[None], (n_space, PAD // 2, LANES))
     slabs = lax.all_to_all(spread, "space", split_axis=0, concat_axis=0, tiled=True)
-    gram = unpack_gram(jnp.sum(slabs, axis=0) / total_cells)[None]
+    gram = unpack_gram(jnp.sum(slabs.astype(jnp.float32), axis=0) / total_cells)[None]
     return (spectra, gram)
 
 

time: 146 us -> 146 us (level)
  no operation moved by 1% of the time
where the time goes in v7:
time: 146 us; the launch traced here: 145 us
  waiting for transfers between devices  54.1 us (37%)
  blocking collectives  47 us (32%)
  starting transfers between devices  25.2 us (17%)
  local copies, waits for them, and re-layouts  7.09 us (5%)
  Pallas kernels  6.16 us (4%)
  other arithmetic  3.77 us (3%)
  between operations  2.1 us (1%)
    all_to_all x1, blocking collectives, per_device(): lax.all_to_all(message, 'freq', split_axis=0, concat_axis=0, tiled=True,...  47 us
    all_to_all x1, waiting for transfers between devices, per_device(): lax.all_to_all(series, 'freq', split_axis=1, concat_axis=0, tiled=True, a...  46.9 us
    all_to_all x1, starting transfers between devices, per_device(): lax.all_to_all(series, 'freq', split_axis=1, concat_axis=0, tiled=True, a...  18.2 us
    pallas_call x1, Pallas kernels, transform_and_gram(): pl.pallas_call(functools.partial(middle_kernel, n_out), out_shape=jax.Sha...  6.16 us
    all_to_all x1, starting transfers between devices, per_device(): lax.all_to_all(spread, 'space', split_axis=0, concat_axis=0, tiled=True)  5.11 us
    all_to_all x1, waiting for transfers between devices, per_device(): lax.all_to_all(spread, 'space', split_axis=0, concat_axis=0, tiled=True)  4.59 us
  transfers between devices with their start and end apart: 3, of which 3 were waited for; matrix products, arithmetic and copies ran while one was open for 4% of the time, Pallas kernels for 0%

profile of v7, /device:TPU:4, one launch (start us, length us, event | category | flops | bytes accessed | tf_op | source)
XLA Modules:
  0.0 145.5 jit_solution(2154468219750073299)
XLA Ops:
  0.6 2.3 %copy.23 = bf16[4,32,8,512]{3,2,0,1:T(8,128)(2,1)} copy(bf16[4,32,8,512]{3,2,1,0:T(8,128)(2,1)} %bitcast.37) | data formatting | bytes 2097152 | tf_op jit(solution)/shard_map/all_to_all | solution.py:139
  3.0 18.2 %all-to-all-start = ((bf16[32,32,512]{2,0,1:T(8,128)(2,1)}), bf16[32,32,512]{2,0,1:T(8,128)(2,1)S(1)}, u32[]{:S(2)}, u32[]{:S(2)}) async-start(bf16[32,32,512]{2,0,1:T(8,128)(2,1)} %bitcast.31), calls=%async_computation | async-start | bytes 2097152 | tf_op jit(solution)/shard_map/all_to_all | solution.py:139
  21.2 0.0 copy-start
  21.2 0.6 copy-done
  21.8 0.1 slice.22
  22.0 0.1 slice.21
  22.1 0.7 multiply_reduce_fusion
  24.1 0.0 copy-start.1
  24.1 0.6 copy-done.1
  24.8 0.1 pad_add_fusion.scalars_ref
  24.9 0.1 add_select_fusion.2
  25.0 2.7 %multiply_convert_fusion = (bf16[1,9,32,512]{3,2,1,0:T(8,128)(2,1)S(1)}, bf16[1,9,32,512]{3,2,1,0:T(8,128)(2,1)S(1)}) fusion(s32[9,32]{1,0:T(8,128)S(1)} %add_select_fusion.2, f32[512]{0:T(512)S(1)} %fusion.11), kind=kLoop, calls=%fused_computation.9 | loop fusion | flops 2801664 | bytes 593024 | tf_op jit(solution)/shard_map/convert.1
  27.7 0.1 pad_maximum_fusion
  27.8 46.9 %all-to-all-done = bf16[32,32,512]{2,0,1:T(8,128)(2,1)S(1)} async-done(((bf16[32,32,512]{2,0,1:T(8,128)(2,1)}), bf16[32,32,512]{2,0,1:T(8,128)(2,1)S(1)}, u32[]{:S(2)}, u32[]{:S(2)}) %all-to-all-start) | async-done | bytes 1048608 | tf_op jit(solution)/shard_map/all_to_all | solution.py:139
  74.7 1.9 %collective-permute-start = (bf16[1024,512]{1,0:T(8,128)(2,1)S(1)}, bf16[1024,512]{1,0:T(8,128)(2,1)S(1)}, u32[]{:S(2)}, u32[]{:S(2)}) collective-permute-start(bf16[1024,512]{1,0:T(8,128)(2,1)S(1)} %bitcast.33), channel_id=1, source_target_pairs={{0,8},{8,0},{16,24},{24,16},{32,40},{40,32},{48,56},{56,48},{64,72... | collective-permute-start | bytes 3145736 | tf_op jit(solution)/shard_map/ppermute | solution.py:146
  76.6 2.6 %collective-permute-done.other_ref = bf16[1024,512]{1,0:T(8,128)(2,1)S(1)} collective-permute-done((bf16[1024,512]{1,0:T(8,128)(2,1)S(1)}, bf16[1024,512]{1,0:T(8,128)(2,1)S(1)}, u32[]{:S(2)}, u32[]{:S(2)}) %collective-permute-start) | collective-permute-done | bytes 1048608 | tf_op jit(solution)/shard_map/ppermute | solution.py:146
  79.2 6.2 %transform_and_gram.1 = bf16[32,88,128]{2,1,0:T(8,128)(2,1)S(1)} custom-call(s32[8]{0:T(128)S(1)} %pad_add_fusion.scalars_ref, bf16[1024,512]{1,0:T(8,128)(2,1)S(1)} %bitcast.34, bf16[1024,512]{1,0:T(8,128)(2,1)S(1)} %collective-permute-done.other_ref, bf16[576,512]{1,0:T(8,128)(2,1)S(1)} %bitcast.35), custom_call_target="tpu_custom_call" | custom-call | flops 2650800128 | bytes 4194304 | tf_op jit(solution)/shard_map/transform_and_gram/pallas_call | solution.py:103
  85.4 47.0 %all_to_all.29 = bf16[32,88,128]{2,1,0:T(8,128)(2,1)S(1)} all-to-all(bf16[32,88,128]{2,1,0:T(8,128)(2,1)S(1)} %transform_and_gram.1), channel_id=1, replica_groups={{0,16,32,48,64,80,96,112,128,144,160,176,192,208,224,240,256,272,288,30..., dimensions={0} | all-to-all | bytes 1441792 | tf_op jit(solution)/shard_map/all_to_all | solution.py:148
  132.5 0.6 broadcast_in_dim.10
  133.1 5.1 %all-to-all-start.2 = ((bf16[8,32,128]{2,1,0:T(8,128)(2,1)}), bf16[8,32,128]{2,1,0:T(8,128)(2,1)S(1)}, u32[]{:S(2)}, u32[]{:S(2)}) async-start(bf16[8,32,128]{2,1,0:T(8,128)(2,1)} %broadcast_in_dim.10), calls=%async_computation.2 | async-start | bytes 131072 | tf_op jit(solution)/shard_map/all_to_all | solution.py:155
  138.2 0.3 reshape.129
  138.6 0.3 copy.18
  138.9 1.1 reshape.130
  140.0 4.6 %all-to-all-done.2 = bf16[8,32,128]{2,1,0:T(8,128)(2,1)S(1)} async-done(((bf16[8,32,128]{2,1,0:T(8,128)(2,1)}), bf16[8,32,128]{2,1,0:T(8,128)(2,1)S(1)}, u32[]{:S(2)}, u32[]{:S(2)}) %all-to-all-start.2) | async-done | bytes 65568 | tf_op jit(solution)/shard_map/all_to_all | solution.py:155
  144.6 0.1 fusion.12
  144.7 0.1 copy.19
  144.8 0.7 copy.20
  (10 shorter events, 0.2 us)
Async XLA Ops:
  3.0 71.7 %all-to-all-start = ((bf16[32,32,512]{2,0,1:T(8,128)(2,1)}), bf16[32,32,512]{2,0,1:T(8,128)(2,1)S(1)}, u32[]{:S(2)}, u32[]{:S(2)}) async-start(bf16[32,32,512]{2,0,1:T(8,128)(2,1)} %bitcast.31), calls=%async_computation | async-start | bytes 2097152 | tf_op jit(solution)/shard_map/all_to_all | solution.py:139
  21.2 0.7 copy-start
  24.1 0.7 copy-start.1
  74.7 4.5 %collective-permute-start = (bf16[1024,512]{1,0:T(8,128)(2,1)S(1)}, bf16[1024,512]{1,0:T(8,128)(2,1)S(1)}, u32[]{:S(2)}, u32[]{:S(2)}) collective-permute-start(bf16[1024,512]{1,0:T(8,128)(2,1)S(1)} %bitcast.33), channel_id=1, source_target_pairs={{0,8},{8,0},{16,24},{24,16},{32,40},{40,32},{48,56},{56,48},{64,72... | collective-permute-start | bytes 3145736 | tf_op jit(solution)/shard_map/ppermute | solution.py:146
  133.1 11.5 %all-to-all-start.2 = ((bf16[8,32,128]{2,1,0:T(8,128)(2,1)}), bf16[8,32,128]{2,1,0:T(8,128)(2,1)S(1)}, u32[]{:S(2)}, u32[]{:S(2)}) async-start(bf16[8,32,128]{2,1,0:T(8,128)(2,1)} %broadcast_in_dim.10), calls=%async_computation.2 | async-start | bytes 131072 | tf_op jit(solution)/shard_map/all_to_all | solution.py:155

commit v8 on v7

--- a/solution.py
+++ b/solution.py
@@ -35,7 +35,8 @@
     return jnp.stack([real_part, imag_part], axis=0).astype(jnp.bfloat16)
 
 
-def middle_kernel(n_out, scalars_ref, mine_ref, other_ref, table_ref, out_ref, rows32, spec32, own32):
+def middle_kernel(n_out, piece_rows, scalars_ref, mine_ref, other_ref, table_ref, own_ref, gram_ref,
+                  rows32, spec32, own32, gram32):
     quarters, spread_rows, _ = rows32.shape
     own_rows = OWN * quarters
     run = spread_rows // SPREAD // (2 * n_out)
@@ -88,27 +89,35 @@
         merged = jnp.where(keep, both, pltpu.roll(both, PAD, 1))
         packed = jnp.where(low_half, merged[: PAD // 2], merged[PAD // 2 :])
         own = own32[pl.ds(pl.multiple_of(j * own_rows, 8), own_rows), :]
-        out_ref[j] = jnp.concatenate([own, packed], axis=0).astype(jnp.bfloat16)
+        own_ref[j] = own.astype(jnp.bfloat16)
+        for p in range(PAD // 2 // piece_rows):
+            target = (p * n_out + j) * piece_rows
+            gram32[pl.ds(target, piece_rows), :] = packed[p * piece_rows : (p + 1) * piece_rows]
         return carry
 
     lax.fori_loop(0, n_out, one_frequency, 0, unroll=16)
+    gram_ref[...] = gram32[...].astype(jnp.bfloat16)
 
 
-def transform_and_gram(scalars, mine, other, table, n_out):
+def transform_and_gram(scalars, mine, other, table, n_out, piece_rows):
     run_rows, cells = mine.shape
     quarters = cells // LANES
     own_rows = OWN * quarters
     vmem = pl.BlockSpec(memory_space=pltpu.VMEM)
     flops = 2 * NBLK * table.shape[0] * NFFT * cells + 2 * n_out * (2 * PAD) ** 2 * cells
     return pl.pallas_call(
-        functools.partial(middle_kernel, n_out),
-        out_shape=jax.ShapeDtypeStruct((n_out, own_rows + PAD // 2, LANES), jnp.bfloat16),
+        functools.partial(middle_kernel, n_out, piece_rows),
+        out_shape=(
+            jax.ShapeDtypeStruct((n_out, own_rows, LANES), jnp.bfloat16),
+            jax.ShapeDtypeStruct((n_out * PAD // 2, LANES), jnp.bfloat16),
+        ),
         in_specs=[pl.BlockSpec(memory_space=pltpu.SMEM), vmem, vmem, vmem],
-        out_specs=vmem,
+        out_specs=(vmem, vmem),
         scratch_shapes=[
             pltpu.VMEM((quarters, 2 * run_rows * SPREAD, LANES), jnp.float32),
             pltpu.VMEM((quarters, n_out * SPAN, LANES), jnp.float32),
             pltpu.VMEM((n_out * own_rows, LANES), jnp.float32),
+            pltpu.VMEM((n_out * PAD // 2, LANES), jnp.float32),
         ],
         cost_estimate=pl.CostEstimate(flops=flops, bytes_accessed=4 << 20, transcendentals=0),
         compiler_params=pltpu.CompilerParams(vmem_limit_bytes=32 << 20),
@@ -133,6 +142,7 @@
     total_cells = slab_cells * n_space
     cells = slab_cells // n_out
     quarters = cells // LANES
+    piece_rows = PAD // 2 // n_space
     core = lax.rem(lax.axis_index("freq"), 2)
     same_core = [[2 * chip + side for chip in range(n_out)] for side in range(2)]
 
@@ -144,16 +154,20 @@
     scalars = jnp.concatenate([starts, core[None].astype(starts.dtype)])
     mine, table, scalars = lax.optimization_barrier((mine, table, scalars))
     other = lax.ppermute(mine, "freq", [(index, index ^ 1) for index in range(n_freq)])
-    message = transform_and_gram(scalars, mine, other, table, n_out)
+    own, partial = transform_and_gram(scalars, mine, other, table, n_out, piece_rows)
+    partial = partial.reshape(n_space, n_out * piece_rows, LANES)
+    gathered = lax.all_to_all(partial, "space", split_axis=0, concat_axis=0, tiled=True)
+    piece_sum = jnp.sum(gathered.astype(jnp.float32), axis=0).astype(jnp.bfloat16)
+    message = jnp.concatenate([own, piece_sum.reshape(n_out, piece_rows, LANES)], axis=1)
     received = lax.all_to_all(
         message, "freq", split_axis=0, concat_axis=0, tiled=True, axis_index_groups=same_core
     )
     own = received[:, : OWN * quarters].reshape(n_out, PARTS, NBLK, cells)
     spectra = jnp.transpose(own, (1, 2, 0, 3)).reshape(1, PARTS, NBLK, slab_cells)
-    slab_gram = jnp.sum(received[:, OWN * quarters :].astype(jnp.float32), axis=0).astype(jnp.bfloat16)
-    spread = jnp.broadcast_to(slab_gram[None], (n_space, PAD // 2, LANES))
-    slabs = lax.all_to_all(spread, "space", split_axis=0, concat_axis=0, tiled=True)
-    gram = unpack_gram(jnp.sum(slabs.astype(jnp.float32), axis=0) / total_cells)[None]
+    gram_piece = jnp.sum(received[:, OWN * quarters :].astype(jnp.float32), axis=0)
+    spread = jnp.broadcast_to(gram_piece[None], (n_space, piece_rows, LANES))
+    pieces = lax.all_to_all(spread, "space", split_axis=0, concat_axis=0, tiled=True)
+    gram = unpack_gram(pieces.reshape(PAD // 2, LANES) / total_cells)[None]
     return (spectra, gram)
 
 

time: 146 us -> 148 us (1.014)
  blocking collectives: 47 us -> 50.5 us
    all_to_all x0 -> x1, blocking collectives: none -> 12.4 us  [per_device(): lax.all_to_all(partial, 'space', split_axis=0, concat_axis=0, tiled=True)]
    all_to_all x1, blocking collectives: 47 us -> 38.1 us  [per_device(): lax.all_to_all(message, 'freq', split_axis=0, concat_axis=0, tiled=True,...]
where the time goes in v8:
time: 148 us
  waiting for transfers between devices  54 us (36%)
  blocking collectives  50.5 us (34%)
  starting transfers between devices  23.8 us (16%)
  local copies, waits for them, and re-layouts  6.46 us (4%)
  Pallas kernels  6.2 us (4%)
  other arithmetic  4.54 us (3%)
  between operations  2.11 us (1%)
    all_to_all x1, waiting for transfers between devices, per_device(): lax.all_to_all(series, 'freq', split_axis=1, concat_axis=0, tiled=True, a...  46.9 us
    all_to_all x1, blocking collectives, per_device(): lax.all_to_all(message, 'freq', split_axis=0, concat_axis=0, tiled=True,...  38.1 us
    all_to_all x1, starting transfers between devices, per_device(): lax.all_to_all(series, 'freq', split_axis=1, concat_axis=0, tiled=True, a...  18.2 us
    all_to_all x1, blocking collectives, per_device(): lax.all_to_all(partial, 'space', split_axis=0, concat_axis=0, tiled=True)  12.4 us
    pallas_call x1, Pallas kernels, transform_and_gram(): pl.pallas_call(functools.partial(middle_kernel, n_out, piece_rows), out_s...  6.2 us
    all_to_all x1, waiting for transfers between devices, per_device(): lax.all_to_all(spread, 'space', split_axis=0, concat_axis=0, tiled=True)  4.46 us
    all_to_all x1, starting transfers between devices, per_device(): lax.all_to_all(spread, 'space', split_axis=0, concat_axis=0, tiled=True)  3.66 us
  transfers between devices with their start and end apart: 3, of which 3 were waited for; matrix products, arithmetic and copies ran while one was open for 4% of the time, Pallas kernels for 0%

profile of v8, /device:TPU:4, one launch (start us, length us, event | category | flops | bytes accessed | tf_op | source)
XLA Modules:
  0.0 147.6 jit_solution(5857905653291059590)
XLA Ops:
  0.6 2.3 %copy.19 = bf16[4,32,8,512]{3,2,0,1:T(8,128)(2,1)} copy(bf16[4,32,8,512]{3,2,1,0:T(8,128)(2,1)} %bitcast.37) | data formatting | bytes 2097152 | tf_op jit(solution)/shard_map/all_to_all | solution.py:149
  3.0 18.2 %all-to-all-start = ((bf16[32,32,512]{2,0,1:T(8,128)(2,1)}), bf16[32,32,512]{2,0,1:T(8,128)(2,1)S(1)}, u32[]{:S(2)}, u32[]{:S(2)}) async-start(bf16[32,32,512]{2,0,1:T(8,128)(2,1)} %bitcast.30), calls=%async_computation | async-start | bytes 2097152 | tf_op jit(solution)/shard_map/all_to_all | solution.py:149
  21.2 0.0 copy-start
  21.2 0.6 copy-done
  21.8 0.1 slice.22
  22.0 0.1 slice.21
  22.1 0.7 multiply_reduce_fusion
  24.1 0.0 copy-start.1
  24.1 0.6 copy-done.1
  24.8 0.1 pad_add_fusion.scalars_ref
  24.9 0.1 add_select_fusion.2
  25.0 2.7 %multiply_convert_fusion = (bf16[1,9,32,512]{3,2,1,0:T(8,128)(2,1)S(1)}, bf16[1,9,32,512]{3,2,1,0:T(8,128)(2,1)S(1)}) fusion(s32[9,32]{1,0:T(8,128)S(1)} %add_select_fusion.2, f32[512]{0:T(512)S(1)} %fusion.10), kind=kLoop, calls=%fused_computation.9 | loop fusion | flops 2801664 | bytes 593024 | tf_op jit(solution)/shard_map/convert.1
  27.7 0.1 pad_maximum_fusion
  27.8 46.9 %all-to-all-done = bf16[32,32,512]{2,0,1:T(8,128)(2,1)S(1)} async-done(((bf16[32,32,512]{2,0,1:T(8,128)(2,1)}), bf16[32,32,512]{2,0,1:T(8,128)(2,1)S(1)}, u32[]{:S(2)}, u32[]{:S(2)}) %all-to-all-start) | async-done | bytes 1048608 | tf_op jit(solution)/shard_map/all_to_all | solution.py:149
  74.7 1.9 %collective-permute-start = (bf16[1024,512]{1,0:T(8,128)(2,1)S(1)}, bf16[1024,512]{1,0:T(8,128)(2,1)S(1)}, u32[]{:S(2)}, u32[]{:S(2)}) collective-permute-start(bf16[1024,512]{1,0:T(8,128)(2,1)S(1)} %bitcast.32), channel_id=1, source_target_pairs={{0,8},{8,0},{16,24},{24,16},{32,40},{40,32},{48,56},{56,48},{64,72... | collective-permute-start | bytes 3145736 | tf_op jit(solution)/shard_map/ppermute | solution.py:156
  76.6 2.6 %collective-permute-done.other_ref = bf16[1024,512]{1,0:T(8,128)(2,1)S(1)} collective-permute-done((bf16[1024,512]{1,0:T(8,128)(2,1)S(1)}, bf16[1024,512]{1,0:T(8,128)(2,1)S(1)}, u32[]{:S(2)}, u32[]{:S(2)}) %collective-permute-start) | collective-permute-done | bytes 1048608 | tf_op jit(solution)/shard_map/ppermute | solution.py:156
  79.2 6.2 %transform_and_gram.1 = (bf16[32,56,128]{2,1,0:T(8,128)(2,1)S(1)}, bf16[1024,128]{1,0:T(8,128)(2,1)S(1)}) custom-call(s32[8]{0:T(128)S(1)} %pad_add_fusion.scalars_ref, bf16[1024,512]{1,0:T(8,128)(2,1)S(1)} %bitcast.33, bf16[1024,512]{1,0:T(8,128)(2,1)S(1)} %collective-permute-done.other_ref, bf16[576,512]{1,0:T(8,128)(2,1)S(1)} %bitcast.34), custom_call_target="tpu_custom_call" | custom-call | flops 2650800128 | bytes 4194304 | tf_op jit(solution)/shard_map/transform_and_gram/pallas_call | solution.py:108
  85.4 12.4 %all_to_all.34 = bf16[8,128,128]{2,1,0:T(8,128)(2,1)S(1)} all-to-all(bf16[8,128,128]{2,1,0:T(8,128)(2,1)S(1)} %bitcast.35), channel_id=1, replica_groups=mesh['freq'=64,'space'=8] {'space'}, dimensions={0} | all-to-all | bytes 524288 | tf_op jit(solution)/shard_map/all_to_all | solution.py:159
  97.9 0.1 pad_maximum_fusion.1
  98.0 38.1 %all_to_all.35 = bf16[32,60,128]{2,1,0:T(8,128)(2,1)S(1)} all-to-all(bf16[32,60,128]{2,1,0:T(8,128)(2,1)S(1)} %pad_maximum_fusion.1), channel_id=1, replica_groups={{0,16,32,48,64,80,96,112,128,144,160,176,192,208,224,240,256,272,288,30..., dimensions={0} | all-to-all | bytes 983040 | tf_op jit(solution)/shard_map/all_to_all | solution.py:162
  136.1 0.6 broadcast_in_dim.10
  136.7 3.7 %all-to-all-start.3 = ((f32[8,4,128]{2,1,0:T(4,128)}), f32[8,4,128]{2,1,0:T(4,128)S(1)}, u32[]{:S(2)}, u32[]{:S(2)}) async-start(f32[8,4,128]{2,1,0:T(4,128)} %broadcast_in_dim.10), calls=%async_computation.3 | async-start | bytes 32768 | tf_op jit(solution)/shard_map/all_to_all | solution.py:169
  140.4 0.3 reshape.140
  140.7 0.3 copy.14
  141.0 1.1 reshape.141
  142.1 4.5 %all-to-all-done.3 = f32[8,4,128]{2,1,0:T(4,128)S(1)} async-done(((f32[8,4,128]{2,1,0:T(4,128)}), f32[8,4,128]{2,1,0:T(4,128)S(1)}, u32[]{:S(2)}, u32[]{:S(2)}) %all-to-all-start.3) | async-done | bytes 16416 | tf_op jit(solution)/shard_map/all_to_all | solution.py:169
  146.6 0.1 fusion.11
  146.7 0.1 copy.15
  146.9 0.7 maximum_bitcast_fusion
  (11 shorter events, 0.3 us)
Async XLA Ops:
  3.0 71.7 %all-to-all-start = ((bf16[32,32,512]{2,0,1:T(8,128)(2,1)}), bf16[32,32,512]{2,0,1:T(8,128)(2,1)S(1)}, u32[]{:S(2)}, u32[]{:S(2)}) async-start(bf16[32,32,512]{2,0,1:T(8,128)(2,1)} %bitcast.30), calls=%async_computation | async-start | bytes 2097152 | tf_op jit(solution)/shard_map/all_to_all | solution.py:149
  21.2 0.7 copy-start
  24.1 0.7 copy-start.1
  74.7 4.5 %collective-permute-start = (bf16[1024,512]{1,0:T(8,128)(2,1)S(1)}, bf16[1024,512]{1,0:T(8,128)(2,1)S(1)}, u32[]{:S(2)}, u32[]{:S(2)}) collective-permute-start(bf16[1024,512]{1,0:T(8,128)(2,1)S(1)} %bitcast.32), channel_id=1, source_target_pairs={{0,8},{8,0},{16,24},{24,16},{32,40},{40,32},{48,56},{56,48},{64,72... | collective-permute-start | bytes 3145736 | tf_op jit(solution)/shard_map/ppermute | solution.py:156
  136.7 9.9 %all-to-all-start.3 = ((f32[8,4,128]{2,1,0:T(4,128)}), f32[8,4,128]{2,1,0:T(4,128)S(1)}, u32[]{:S(2)}, u32[]{:S(2)}) async-start(f32[8,4,128]{2,1,0:T(4,128)} %broadcast_in_dim.10), calls=%async_computation.3 | async-start | bytes 32768 | tf_op jit(solution)/shard_map/all_to_all | solution.py:169

commit v9 on v6

--- a/solution.py
+++ b/solution.py
@@ -40,6 +40,16 @@
     own_rows = OWN * quarters
     run = spread_rows // SPREAD // (2 * n_out)
     core = scalars_ref[NBLK]
+    even = core == 0
+
+    def aligned_rows(first_row):
+        pieces = []
+        for source in range(first_row // (2 * run), (first_row + NFFT) // (2 * run)):
+            taken = slice(source * run, (source + 1) * run)
+            mine, other = mine_ref[taken, :], other_ref[taken, :]
+            pieces += [jnp.where(even, mine, other), jnp.where(even, other, mine)]
+        return jnp.concatenate(pieces, axis=0)
+
     for quarter in range(quarters):
         lanes = slice(quarter * LANES, (quarter + 1) * LANES)
         for source in range(n_out):
@@ -53,9 +63,14 @@
 
     for block in range(NBLK):
         first = scalars_ref[block] * SPREAD
-        block_rows = jnp.concatenate(
-            [rows32[quarter, pl.ds(first, NFFT, stride=SPREAD), :] for quarter in range(quarters)], axis=1
-        ).astype(jnp.bfloat16)
+        if block == 0:
+            block_rows = aligned_rows(0)
+        elif block == NBLK - 1:
+            block_rows = aligned_rows(2 * run * n_out - NFFT)
+        else:
+            block_rows = jnp.concatenate(
+                [rows32[quarter, pl.ds(first, NFFT, stride=SPREAD), :] for quarter in range(quarters)], axis=1
+            ).astype(jnp.bfloat16)
         spec = jnp.dot(table_ref[...], block_rows, preferred_element_type=jnp.float32)
         for part in range(PARTS):
             for shift in range(SHIFTS):
@@ -116,6 +131,25 @@
     )(scalars, mine, other, table)
 
 
+def split_kernel(series_ref, chunks_ref):
+    count, _, cells = chunks_ref.shape
+    for chunk in range(count):
+        chunks_ref[chunk] = series_ref[:, chunk * cells : (chunk + 1) * cells]
+
+
+def split_cells(series, n_chunks):
+    rows, slab_cells = series.shape
+    cells, step = slab_cells // n_chunks, n_chunks // 2
+    return pl.pallas_call(
+        split_kernel,
+        grid=(2,),
+        out_shape=jax.ShapeDtypeStruct((n_chunks, rows, cells), series.dtype),
+        in_specs=[pl.BlockSpec((rows, step * cells), lambda i: (0, i))],
+        out_specs=pl.BlockSpec((step, rows, cells), lambda i: (i, 0, 0)),
+        name="split_cells",
+    )(series)
+
+
 def unpack_gram(packed):
     square = jnp.concatenate([packed[:, :PAD], packed[:, PAD:]], axis=0)[:ORDER, :ORDER]
     upper = jnp.arange(ORDER)[:, None] <= jnp.arange(ORDER)[None, :]
@@ -137,8 +171,8 @@
     same_core = [[2 * chip + side for chip in range(n_out)] for side in range(2)]
 
     mine = lax.all_to_all(
-        series, "freq", split_axis=1, concat_axis=0, tiled=True, axis_index_groups=same_core
-    )
+        split_cells(series, n_out), "freq", split_axis=0, concat_axis=0, tiled=True, axis_index_groups=same_core
+    ).reshape(-1, cells)
     own_freqs = jnp.where(core == 0, freqs[0::2], freqs[1::2])
     table = transform_table(own_freqs, alpha).reshape(PARTS * SHIFTS * n_out, NFFT)
     scalars = jnp.concatenate([starts, core[None].astype(starts.dtype)])

time: 146 us -> 146 us (level)
  local copies, waits for them, and re-layouts: 7.12 us -> 4.77 us
  Pallas kernels: 6.16 us -> 8.11 us
    all_to_all x1 -> x0, local copies, waits for them, and re-layouts: 2.34 us -> none  [per_device(): lax.all_to_all(series, 'freq', split_axis=1, concat_axis=0, tiled=True, a...]
    pallas_call x0 -> x1, Pallas kernels: none -> 2.06 us  [split_cells(): pl.pallas_call(split_kernel, grid=(2,), out_shape=jax.ShapeDtypeStruct((n...]
where the time goes in v9:
time: 146 us; the launch traced here: 145 us
  waiting for transfers between devices  54.3 us (37%)
  blocking collectives  47 us (32%)
  starting transfers between devices  25.2 us (17%)
  Pallas kernels  8.11 us (6%)
  local copies, waits for them, and re-layouts  4.77 us (3%)
  other arithmetic  3.77 us (3%)
  between operations  2.1 us (1%)
    all_to_all x1, blocking collectives, per_device(): lax.all_to_all(message, 'freq', split_axis=0, concat_axis=0, tiled=True,...  47 us
    all_to_all x1, waiting for transfers between devices, per_device(): lax.all_to_all(split_cells(series, n_out), 'freq', split_axis=0, concat_a...  46.9 us
    all_to_all x1, starting transfers between devices, per_device(): lax.all_to_all(split_cells(series, n_out), 'freq', split_axis=0, concat_a...  18.2 us
    pallas_call x1, Pallas kernels, transform_and_gram(): pl.pallas_call(functools.partial(middle_kernel, n_out), out_shape=jax.Sha...  6.05 us
    all_to_all x1, starting transfers between devices, per_device(): lax.all_to_all(spread, 'space', split_axis=0, concat_axis=0, tiled=True)  5.11 us
    all_to_all x1, waiting for transfers between devices, per_device(): lax.all_to_all(spread, 'space', split_axis=0, concat_axis=0, tiled=True)  4.82 us
  transfers between devices with their start and end apart: 3, of which 3 were waited for; matrix products, arithmetic and copies ran while one was open for 4% of the time, Pallas kernels for 0%

profile of v9, /device:TPU:4, one launch (start us, length us, event | category | flops | bytes accessed | tf_op | source)
XLA Modules:
  0.0 145.3 jit_solution(5881547114247546399)
XLA Ops:
  0.6 2.1 %split_cells.1 = bf16[32,32,512]{2,1,0:T(8,128)(2,1)} custom-call(bf16[32,16384]{1,0:T(8,128)(2,1)} %series_ref.1), custom_call_target="tpu_custom_call" | custom-call | tf_op jit(solution)/shard_map/split_cells/pallas_call | solution.py:143
  2.7 18.2 %all-to-all-start = ((bf16[32,32,512]{2,1,0:T(8,128)(2,1)}), bf16[32,32,512]{2,1,0:T(8,128)(2,1)S(1)}, u32[]{:S(2)}, u32[]{:S(2)}) async-start(bf16[32,32,512]{2,1,0:T(8,128)(2,1)} %split_cells.1), calls=%async_computation | async-start | bytes 2097152 | tf_op jit(solution)/shard_map/all_to_all | solution.py:173
  20.9 0.0 copy-start
  20.9 0.6 copy-done
  21.6 0.1 slice.22
  21.7 0.1 slice.21
  21.8 0.7 multiply_reduce_fusion
  23.8 0.0 copy-start.1
  23.8 0.6 copy-done.1
  24.5 0.1 pad_add_fusion.scalars_ref
  24.6 0.1 add_select_fusion.2
  24.7 2.7 %multiply_convert_fusion = (bf16[1,9,32,512]{3,2,1,0:T(8,128)(2,1)S(1)}, bf16[1,9,32,512]{3,2,1,0:T(8,128)(2,1)S(1)}) fusion(s32[9,32]{1,0:T(8,128)S(1)} %add_select_fusion.2, f32[512]{0:T(512)S(1)} %fusion.11), kind=kLoop, calls=%fused_computation.8 | loop fusion | flops 2801664 | bytes 593024 | tf_op jit(solution)/shard_map/convert
  27.5 0.1 pad_maximum_fusion
  27.5 46.9 %all-to-all-done = bf16[32,32,512]{2,1,0:T(8,128)(2,1)S(1)} async-done(((bf16[32,32,512]{2,1,0:T(8,128)(2,1)}), bf16[32,32,512]{2,1,0:T(8,128)(2,1)S(1)}, u32[]{:S(2)}, u32[]{:S(2)}) %all-to-all-start) | async-done | bytes 1048608 | tf_op jit(solution)/shard_map/all_to_all | solution.py:173
  74.4 1.9 %collective-permute-start = (bf16[1024,512]{1,0:T(8,128)(2,1)S(1)}, bf16[1024,512]{1,0:T(8,128)(2,1)S(1)}, u32[]{:S(2)}, u32[]{:S(2)}) collective-permute-start(bf16[1024,512]{1,0:T(8,128)(2,1)S(1)} %bitcast.27), channel_id=1, source_target_pairs={{0,8},{8,0},{16,24},{24,16},{32,40},{40,32},{48,56},{56,48},{64,72... | collective-permute-start | bytes 3145736 | tf_op jit(solution)/shard_map/ppermute | solution.py:180
  76.3 2.6 %collective-permute-done.other_ref = bf16[1024,512]{1,0:T(8,128)(2,1)S(1)} collective-permute-done((bf16[1024,512]{1,0:T(8,128)(2,1)S(1)}, bf16[1024,512]{1,0:T(8,128)(2,1)S(1)}, u32[]{:S(2)}, u32[]{:S(2)}) %collective-permute-start) | collective-permute-done | bytes 1048608 | tf_op jit(solution)/shard_map/ppermute | solution.py:180
  78.9 6.0 %transform_and_gram.1 = bf16[32,88,128]{2,1,0:T(8,128)(2,1)S(1)} custom-call(s32[8]{0:T(128)S(1)} %pad_add_fusion.scalars_ref, bf16[1024,512]{1,0:T(8,128)(2,1)S(1)} %bitcast.28, bf16[1024,512]{1,0:T(8,128)(2,1)S(1)} %collective-permute-done.other_ref, bf16[576,512]{1,0:T(8,128)(2,1)S(1)} %bitcast.29), custom_call_target="tpu_custom_call" | custom-call | flops 2650800128 | bytes 4194304 | tf_op jit(solution)/shard_map/transform_and_gram/pallas_call | solution.py:118
  85.0 47.0 %all_to_all.15 = bf16[32,88,128]{2,1,0:T(8,128)(2,1)S(1)} all-to-all(bf16[32,88,128]{2,1,0:T(8,128)(2,1)S(1)} %transform_and_gram.1), channel_id=1, replica_groups={{0,16,32,48,64,80,96,112,128,144,160,176,192,208,224,240,256,272,288,30..., dimensions={0} | all-to-all | bytes 1441792 | tf_op jit(solution)/shard_map/all_to_all | solution.py:182
  132.1 0.6 broadcast_in_dim.10
  132.7 5.1 %all-to-all-start.2 = ((f32[8,32,128]{2,1,0:T(8,128)}), f32[8,32,128]{2,1,0:T(8,128)S(1)}, u32[]{:S(2)}, u32[]{:S(2)}) async-start(f32[8,32,128]{2,1,0:T(8,128)} %broadcast_in_dim.10), calls=%async_computation.2 | async-start | bytes 262144 | tf_op jit(solution)/shard_map/all_to_all | solution.py:189
  137.9 0.3 reshape.130
  138.2 0.3 copy.14
  138.5 1.1 reshape.131
  139.6 4.8 %all-to-all-done.2 = f32[8,32,128]{2,1,0:T(8,128)S(1)} async-done(((f32[8,32,128]{2,1,0:T(8,128)}), f32[8,32,128]{2,1,0:T(8,128)S(1)}, u32[]{:S(2)}, u32[]{:S(2)}) %all-to-all-start.2) | async-done | bytes 131104 | tf_op jit(solution)/shard_map/all_to_all | solution.py:189
  144.4 0.1 fusion.12
  144.5 0.1 copy.15
  144.6 0.7 copy.16
  (10 shorter events, 0.2 us)
Async XLA Ops:
  2.7 71.7 %all-to-all-start = ((bf16[32,32,512]{2,1,0:T(8,128)(2,1)}), bf16[32,32,512]{2,1,0:T(8,128)(2,1)S(1)}, u32[]{:S(2)}, u32[]{:S(2)}) async-start(bf16[32,32,512]{2,1,0:T(8,128)(2,1)} %split_cells.1), calls=%async_computation | async-start | bytes 2097152 | tf_op jit(solution)/shard_map/all_to_all | solution.py:173
  20.9 0.7 copy-start
  23.8 0.7 copy-start.1
  74.4 4.5 %collective-permute-start = (bf16[1024,512]{1,0:T(8,128)(2,1)S(1)}, bf16[1024,512]{1,0:T(8,128)(2,1)S(1)}, u32[]{:S(2)}, u32[]{:S(2)}) collective-permute-start(bf16[1024,512]{1,0:T(8,128)(2,1)S(1)} %bitcast.27), channel_id=1, source_target_pairs={{0,8},{8,0},{16,24},{24,16},{32,40},{40,32},{48,56},{56,48},{64,72... | collective-permute-start | bytes 3145736 | tf_op jit(solution)/shard_map/ppermute | solution.py:180
  132.7 11.7 %all-to-all-start.2 = ((f32[8,32,128]{2,1,0:T(8,128)}), f32[8,32,128]{2,1,0:T(8,128)S(1)}, u32[]{:S(2)}, u32[]{:S(2)}) async-start(f32[8,32,128]{2,1,0:T(8,128)} %broadcast_in_dim.10), calls=%async_computation.2 | async-start | bytes 262144 | tf_op jit(solution)/shard_map/all_to_all | solution.py:189

commit v10 on v9

--- a/solution.py
+++ b/solution.py
@@ -106,7 +106,7 @@
         out_ref[j] = jnp.concatenate([own, packed], axis=0).astype(jnp.bfloat16)
         return carry
 
-    lax.fori_loop(0, n_out, one_frequency, 0, unroll=16)
+    lax.fori_loop(0, n_out, one_frequency, 0, unroll=32)
 
 
 def transform_and_gram(scalars, mine, other, table, n_out):

time: 146 us -> 145 us (level)
  no operation moved by 1% of the time
where the time goes in v10:
time: 145 us
  waiting for transfers between devices  54.3 us (37%)
  blocking collectives  47 us (32%)
  starting transfers between devices  25.2 us (17%)
  Pallas kernels  7.72 us (5%)
  local copies, waits for them, and re-layouts  4.77 us (3%)
  other arithmetic  3.77 us (3%)
  between operations  2.1 us (1%)
    all_to_all x1, blocking collectives, per_device(): lax.all_to_all(message, 'freq', split_axis=0, concat_axis=0, tiled=True,...  47 us
    all_to_all x1, waiting for transfers between devices, per_device(): lax.all_to_all(split_cells(series, n_out), 'freq', split_axis=0, concat_a...  46.9 us
    all_to_all x1, starting transfers between devices, per_device(): lax.all_to_all(split_cells(series, n_out), 'freq', split_axis=0, concat_a...  18.2 us
    pallas_call x1, Pallas kernels, transform_and_gram(): pl.pallas_call(functools.partial(middle_kernel, n_out), out_shape=jax.Sha...  5.65 us
    all_to_all x1, starting transfers between devices, per_device(): lax.all_to_all(spread, 'space', split_axis=0, concat_axis=0, tiled=True)  5.12 us
    all_to_all x1, waiting for transfers between devices, per_device(): lax.all_to_all(spread, 'space', split_axis=0, concat_axis=0, tiled=True)  4.82 us
  transfers between devices with their start and end apart: 3, of which 3 were waited for; matrix products, arithmetic and copies ran while one was open for 4% of the time, Pallas kernels for 0%

profile of v10, /device:TPU:4, one launch (start us, length us, event | category | flops | bytes accessed | tf_op | source)
XLA Modules:
  0.0 145.0 jit_solution(10261411919214065895)
XLA Ops:
  0.6 2.1 %split_cells.1 = bf16[32,32,512]{2,1,0:T(8,128)(2,1)} custom-call(bf16[32,16384]{1,0:T(8,128)(2,1)} %series_ref.1), custom_call_target="tpu_custom_call" | custom-call | tf_op jit(solution)/shard_map/split_cells/pallas_call | solution.py:143
  2.7 18.2 %all-to-all-start = ((bf16[32,32,512]{2,1,0:T(8,128)(2,1)}), bf16[32,32,512]{2,1,0:T(8,128)(2,1)S(1)}, u32[]{:S(2)}, u32[]{:S(2)}) async-start(bf16[32,32,512]{2,1,0:T(8,128)(2,1)} %split_cells.1), calls=%async_computation | async-start | bytes 2097152 | tf_op jit(solution)/shard_map/all_to_all | solution.py:173
  20.9 0.0 copy-start
  20.9 0.6 copy-done
  21.6 0.1 slice.22
  21.7 0.1 slice.21
  21.8 0.7 multiply_reduce_fusion
  23.8 0.0 copy-start.1
  23.8 0.6 copy-done.1
  24.5 0.1 pad_add_fusion.scalars_ref
  24.6 0.1 add_select_fusion.2
  24.7 2.7 %multiply_convert_fusion = (bf16[1,9,32,512]{3,2,1,0:T(8,128)(2,1)S(1)}, bf16[1,9,32,512]{3,2,1,0:T(8,128)(2,1)S(1)}) fusion(s32[9,32]{1,0:T(8,128)S(1)} %add_select_fusion.2, f32[512]{0:T(512)S(1)} %fusion.11), kind=kLoop, calls=%fused_computation.8 | loop fusion | flops 2801664 | bytes 593024 | tf_op jit(solution)/shard_map/convert
  27.5 0.1 pad_maximum_fusion
  27.5 46.9 %all-to-all-done = bf16[32,32,512]{2,1,0:T(8,128)(2,1)S(1)} async-done(((bf16[32,32,512]{2,1,0:T(8,128)(2,1)}), bf16[32,32,512]{2,1,0:T(8,128)(2,1)S(1)}, u32[]{:S(2)}, u32[]{:S(2)}) %all-to-all-start) | async-done | bytes 1048608 | tf_op jit(solution)/shard_map/all_to_all | solution.py:173
  74.4 1.9 %collective-permute-start = (bf16[1024,512]{1,0:T(8,128)(2,1)S(1)}, bf16[1024,512]{1,0:T(8,128)(2,1)S(1)}, u32[]{:S(2)}, u32[]{:S(2)}) collective-permute-start(bf16[1024,512]{1,0:T(8,128)(2,1)S(1)} %bitcast.27), channel_id=1, source_target_pairs={{0,8},{8,0},{16,24},{24,16},{32,40},{40,32},{48,56},{56,48},{64,72... | collective-permute-start | bytes 3145736 | tf_op jit(solution)/shard_map/ppermute | solution.py:180
  76.3 2.6 %collective-permute-done.other_ref = bf16[1024,512]{1,0:T(8,128)(2,1)S(1)} collective-permute-done((bf16[1024,512]{1,0:T(8,128)(2,1)S(1)}, bf16[1024,512]{1,0:T(8,128)(2,1)S(1)}, u32[]{:S(2)}, u32[]{:S(2)}) %collective-permute-start) | collective-permute-done | bytes 1048608 | tf_op jit(solution)/shard_map/ppermute | solution.py:180
  78.9 5.7 %transform_and_gram.1 = bf16[32,88,128]{2,1,0:T(8,128)(2,1)S(1)} custom-call(s32[8]{0:T(128)S(1)} %pad_add_fusion.scalars_ref, bf16[1024,512]{1,0:T(8,128)(2,1)S(1)} %bitcast.28, bf16[1024,512]{1,0:T(8,128)(2,1)S(1)} %collective-permute-done.other_ref, bf16[576,512]{1,0:T(8,128)(2,1)S(1)} %bitcast.29), custom_call_target="tpu_custom_call" | custom-call | flops 2650800128 | bytes 4194304 | tf_op jit(solution)/shard_map/transform_and_gram/pallas_call | solution.py:118
  84.6 47.0 %all_to_all.15 = bf16[32,88,128]{2,1,0:T(8,128)(2,1)S(1)} all-to-all(bf16[32,88,128]{2,1,0:T(8,128)(2,1)S(1)} %transform_and_gram.1), channel_id=1, replica_groups={{0,16,32,48,64,80,96,112,128,144,160,176,192,208,224,240,256,272,288,30..., dimensions={0} | all-to-all | bytes 1441792 | tf_op jit(solution)/shard_map/all_to_all | solution.py:182
  131.7 0.6 broadcast_in_dim.10
  132.3 5.1 %all-to-all-start.2 = ((f32[8,32,128]{2,1,0:T(8,128)}), f32[8,32,128]{2,1,0:T(8,128)S(1)}, u32[]{:S(2)}, u32[]{:S(2)}) async-start(f32[8,32,128]{2,1,0:T(8,128)} %broadcast_in_dim.10), calls=%async_computation.2 | async-start | bytes 262144 | tf_op jit(solution)/shard_map/all_to_all | solution.py:189
  137.5 0.3 reshape.130
  137.8 0.3 copy.14
  138.1 1.1 reshape.131
  139.2 4.8 %all-to-all-done.2 = f32[8,32,128]{2,1,0:T(8,128)S(1)} async-done(((f32[8,32,128]{2,1,0:T(8,128)}), f32[8,32,128]{2,1,0:T(8,128)S(1)}, u32[]{:S(2)}, u32[]{:S(2)}) %all-to-all-start.2) | async-done | bytes 131104 | tf_op jit(solution)/shard_map/all_to_all | solution.py:189
  144.1 0.1 fusion.12
  144.1 0.1 copy.15
  144.3 0.7 copy.16
  (10 shorter events, 0.2 us)
Async XLA Ops:
  2.7 71.7 %all-to-all-start = ((bf16[32,32,512]{2,1,0:T(8,128)(2,1)}), bf16[32,32,512]{2,1,0:T(8,128)(2,1)S(1)}, u32[]{:S(2)}, u32[]{:S(2)}) async-start(bf16[32,32,512]{2,1,0:T(8,128)(2,1)} %split_cells.1), calls=%async_computation | async-start | bytes 2097152 | tf_op jit(solution)/shard_map/all_to_all | solution.py:173
  20.9 0.7 copy-start
  23.8 0.7 copy-start.1
  74.4 4.5 %collective-permute-start = (bf16[1024,512]{1,0:T(8,128)(2,1)S(1)}, bf16[1024,512]{1,0:T(8,128)(2,1)S(1)}, u32[]{:S(2)}, u32[]{:S(2)}) collective-permute-start(bf16[1024,512]{1,0:T(8,128)(2,1)S(1)} %bitcast.27), channel_id=1, source_target_pairs={{0,8},{8,0},{16,24},{24,16},{32,40},{40,32},{48,56},{56,48},{64,72... | collective-permute-start | bytes 3145736 | tf_op jit(solution)/shard_map/ppermute | solution.py:180
  132.3 11.7 %all-to-all-start.2 = ((f32[8,32,128]{2,1,0:T(8,128)}), f32[8,32,128]{2,1,0:T(8,128)S(1)}, u32[]{:S(2)}, u32[]{:S(2)}) async-start(f32[8,32,128]{2,1,0:T(8,128)} %broadcast_in_dim.10), calls=%async_computation.2 | async-start | bytes 262144 | tf_op jit(solution)/shard_map/all_to_all | solution.py:189
